TPU v7x, 32 devices: a whole 2x2x4 slice. The times are simulated.
32 devices in a mesh: ctx: 8 (over z, x), head: 4 (over y, core).
Axes of the slice: x: 2, y: 2, z: 4, core: 2. Of those that a mesh axis runs over, the one named last changes fastest.
Arguments:
- queries: bfloat16 [16384, 128], P(('ctx', 'head')), may hold values from -6 to 6
- keys: bfloat16 [16384, 128], P(('ctx', 'head')), may hold values from -0.0625 to 0.0625
- values: bfloat16 [16384, 4096], P('ctx', 'head'), may hold values from -6 to 6
- tier_weight_rows: int32 [8, 16384], P(None, 'ctx'), may hold values from 0 to 15
- level_table: float32 [16, 32], P(None, 'head'), may hold values from 0.1 to 10
Outputs:
- mixed: bfloat16 [16384, 4096], P('ctx', 'head')
All inputs are finite; a program needn't handle non-finite values.
Results may differ from a plain program's by a relative error of at most 0.0049.
Values may be sent and summed in bfloat16 or wider, within the bound.
No kernel may reach another device: no remote copies, remote signals or barrier semaphores. Data moves between devices by JAX's collectives and lax.ppermute only.
A program may use at most 192 MiB of HBM per device.

v0:
```python
import jax
import jax.numpy as jnp
from jax import lax
from jax.sharding import PartitionSpec as P

GROUP = 128


def swapped(value, axis, distance):
    mask = 2**distance
    pairs = [(source, source ^ mask) for source in range(lax.axis_size(axis))]
    return lax.ppermute(value, axis, pairs)


def local(queries, keys, values, tier_weight_rows, level_table):
    q_whole, k_whole = (
        lax.all_gather(queries, "head", axis=0, tiled=True),
        lax.all_gather(keys, "head", axis=0, tiled=True),
    )
    tok_rows = values.shape[0]
    columns = values.shape[1]
    head_count = level_table.shape[1]
    head_width = columns // head_count
    key_width = q_whole.shape[1]
    local_bits = (tok_rows // GROUP).bit_length() - 1
    context_exponent = lax.axis_size("ctx").bit_length() - 1
    classes = jnp.arange(level_table.shape[0], dtype=jnp.int32)
    onehot = (tier_weight_rows[:, :, None] == classes[None, None, :]).astype(jnp.float32)
    weights = jnp.einsum("ltc,ch->lth", onehot, level_table, precision=lax.Precision.HIGHEST)
    share = weights / jnp.sum(weights, axis=0)
    local_state = lax.dot_general(
        k_whole, values, (((0,), (0,)), ((), ())), preferred_element_type=jnp.float32
    )
    me_index = lax.axis_index("ctx")
    subtree = local_state
    sibling_states = []
    for bit in range(context_exponent):
        incoming_partner_sums = swapped(subtree, "ctx", bit)
        mine_bit = me_index >> bit & 1
        sibling_states.append(
            jnp.where(mine_bit == 1, incoming_partner_sums, jnp.zeros_like(incoming_partner_sums))
        )
        subtree = subtree + incoming_partner_sums

    def weigh(part, level):
        scaled = part.reshape(tok_rows, head_count, head_width) * share[level][:, :, None]
        return scaled.reshape(tok_rows, columns)

    groups = tok_rows // GROUP
    q_groups = q_whole.reshape(groups, GROUP, key_width)
    k_groups = k_whole.reshape(groups, GROUP, key_width)
    scores = jnp.einsum("nik,njk->nij", q_groups, k_groups, preferred_element_type=jnp.float32)
    causal = jnp.tril(jnp.ones((GROUP, GROUP), dtype=bool))
    scores = jnp.where(causal[None], scores, 0.0).astype(jnp.bfloat16)
    near = jnp.einsum(
        "nij,njc->nic",
        scores,
        values.reshape(groups, GROUP, columns),
        preferred_element_type=jnp.float32,
    )
    total = weigh(near.reshape(tok_rows, columns), 0)
    for level in range(1, local_bits + 1):
        half = GROUP * 2 ** (level - 1)
        blocks = tok_rows // (2 * half)
        grouped_probe_matrix = k_whole.reshape(blocks, 2, half, key_width)
        grouped_content_matrix = values.reshape(blocks, 2, half, columns)
        query_blocked = q_whole.reshape(blocks, 2, half, key_width)
        cumulative_memory = jnp.einsum(
            "bsk,bsc->bkc",
            grouped_probe_matrix[:, 0],
            grouped_content_matrix[:, 0],
            preferred_element_type=jnp.float32,
        )
        cumulative_memory = cumulative_memory.astype(jnp.bfloat16)
        upper_half_branch = jnp.einsum(
            "bsk,bkc->bsc",
            query_blocked[:, 1],
            cumulative_memory,
            preferred_element_type=jnp.float32,
        )
        part = jnp.stack([jnp.zeros_like(upper_half_branch), upper_half_branch], axis=1).reshape(
            tok_rows, columns
        )
        total = total + weigh(part, level)
    for bit in range(context_exponent):
        cumulative_memory = sibling_states[bit].astype(jnp.bfloat16)
        part = jnp.dot(q_whole, cumulative_memory, preferred_element_type=jnp.float32)
        total = total + weigh(part, 1 + local_bits + bit)
    return total.astype(jnp.bfloat16)


def solution(mesh):
    placed = (
        P(("ctx", "head"), None),
        P(("ctx", "head"), None),
        P("ctx", "head"),
        P(None, "ctx"),
        P(None, "head"),
    )
    return jax.shard_map(
        local, mesh=mesh, in_specs=placed, out_specs=P("ctx", "head"), check_vma=False
    )
```

profile of v0, /device:TPU:0, one launch (start us, length us, event | category | flops | bytes accessed | tf_op | source)
XLA Modules:
  0.0 162.7 jit_solution(10967841442434719350)
XLA Ops:
  0.0 0.0 copy-start
  0.0 9.0 %all_gather.7 = bf16[2048,128]{1,0:T(8,128)(2,1)S(1)} all-gather(bf16[512,128]{1,0:T(8,128)(2,1)} %param.6), channel_id=1, replica_groups=mesh['ctx'=8,'head'=4] {'head'}, dimensions={0}, use_global_device_ids=true | all-gather | bytes 655360 | tf_op jit(solution)/shard_map/all_gather | solution.py:18
  9.0 2.9 %fusion.36 = f32[128,1024]{1,0:T(8,128)S(1)} fusion(bf16[2048,128]{1,0:T(8,128)(2,1)S(1)} %all_gather.7, bf16[2048,1024]{1,0:T(8,128)(2,1)} %param.7), kind=kOutput, calls=%fused_computation.75 | convolution fusion | flops 536870912 | bytes 5242880 | tf_op jit(solution)/shard_map/dot_general | solution.py:31
  12.0 1.6 collective-permute-start
  13.5 7.2 %all_gather.6 = bf16[2048,128]{1,0:T(8,128)(2,1)S(1)} all-gather(bf16[512,128]{1,0:T(8,128)(2,1)} %param.5), channel_id=1, replica_groups=mesh['ctx'=8,'head'=4] {'head'}, dimensions={0}, use_global_device_ids=true | all-gather | bytes 655360 | tf_op jit(solution)/shard_map/all_gather | solution.py:17
  20.7 0.0 copy-done
  20.7 1.3 fusion.35
  22.1 0.8 slice_bitcast_fusion.51
  22.9 4.7 %convolution_bitcast_fusion.2 = f32[4,1,256,1024]{3,2,1,0:T(8,128)} fusion(bf16[4,2,256,1024]{3,2,1,0:T(8,128)(2,1)} %bitcast.185, bf16[4,2,256,128]{3,2,1,0:T(8,128)(2,1)S(1)} %bitcast.200, bf16[4,2,256,128]{3,2,1,0:T(8,128)(2,1)S(1)} %bitcast.195), kind=kOutput, calls=%fused_computation.18 | convolution fusion | flops 537395200 | bytes 6815744 | tf_op jit(solution)/shard_map/bsk,bkc->bsc/dot_general | solution.py:75
  27.6 4.6 %convolution_bitcast_fusion.1 = f32[2,1,512,1024]{3,2,1,0:T(8,128)} fusion(bf16[2,2,512,1024]{3,2,1,0:T(8,128)(2,1)} %bitcast.186, bf16[2,2,512,128]{3,2,1,0:T(8,128)(2,1)S(1)} %bitcast.201, bf16[2,2,512,128]{3,2,1,0:T(8,128)(2,1)S(1)} %bitcast.196), kind=kOutput, calls=%fused_computation.17 | convolution fusion | flops 537133056 | bytes 6815744 | tf_op jit(solution)/shard_map/bsk,bkc->bsc/dot_general | solution.py:75
  32.2 4.7 %convolution_bitcast_fusion = f32[1,1,1024,1024]{3,2,1,0:T(8,128)} fusion(bf16[1,2,1024,1024]{3,2,1,0:T(8,128)(2,1)} %bitcast.187, bf16[1,2,1024,128]{3,2,1,0:T(8,128)(2,1)S(1)} %bitcast.202, bf16[1,2,1024,128]{3,2,1,0:T(8,128)(2,1)S(1)} %bitcast.197), kind=kOutput, calls=%fused_computation.16 | convolution fusion | flops 537001984 | bytes 6815744 | tf_op jit(solution)/shard_map/bsk,bkc->bsc/dot_general | solution.py:75
  36.9 7.0 %fusion.16 = f32[16,128,1024]{2,1,0:T(8,128)} fusion(bf16[16,128,1024]{2,1,0:T(8,128)(2,1)} %bitcast.188, bf16[16,128,128]{2,1,0:T(8,128)(2,1)S(1)} %bitcast.198, bf16[16,128,128]{2,1,0:T(8,128)(2,1)S(1)} %bitcast.203, pred[128,128]{1,0:T(8,128)(4,1)S(1)} %iota_compare_fusion.2), kind=kOutput, calls=%fused_computation.33 | convolution fusion | flops 604504064 | bytes 13647872 | tf_op jit(solution)/shard_map/nij,njc->nic/dot_general | solution.py:55
  43.9 0.0 collective-permute-done
  43.9 0.1 add.40
  43.9 1.6 %collective-permute-start.1 = (f32[128,1024]{1,0:T(8,128)S(1)}, f32[128,1024]{1,0:T(8,128)S(1)}, u32[]{:S(2)}, u32[]{:S(2)}) collective-permute-start(f32[128,1024]{1,0:T(8,128)S(1)} %add.40), channel_id=1, source_target_pairs={{0,8},{4,12},{8,0},{12,4},{16,24},{20,28},{24,16},{28,20},{1,9},{5... | collective-permute-start | bytes 1572872 | tf_op jit(solution)/shard_map/ppermute | solution.py:12
  45.6 4.9 %convolution_bitcast_fusion.3 = f32[8,1,128,1024]{3,2,1,0:T(8,128)} fusion(bf16[8,2,128,1024]{3,2,1,0:T(8,128)(2,1)} %bitcast.189, bf16[8,2,128,128]{3,2,1,0:T(8,128)(2,1)S(1)} %bitcast.204, bf16[8,2,128,128]{3,2,1,0:T(8,128)(2,1)S(1)} %bitcast.199), kind=kOutput, calls=%fused_computation.19 | convolution fusion | flops 537919488 | bytes 6815744 | tf_op jit(solution)/shard_map/bsk,bkc->bsc/dot_general | solution.py:75
  50.4 6.6 %stack.25.clone = f32[8,2,128,1024]{3,2,1,0:T(8,128)} pad(f32[8,1,128,1024]{3,2,1,0:T(8,128)} %convolution_bitcast_fusion.3, f32[]{:T(128)} %constant.6.clone.1), padding=0_0x1_0x0_0x0_0 | pad | bytes 12582916 | tf_op jit(solution)/shard_map/stack | solution.py:81
  57.0 9.2 %copy.12 = f32[2048,1024]{0,1:T(8,128)} copy(f32[2048,1024]{1,0:T(8,128)} %bitcast.192) | data formatting | bytes 16777216 | tf_op jit(solution)/shard_map/reshape;reshape | solution.py:46
  66.2 6.6 %stack.27.clone = f32[4,2,256,1024]{3,2,1,0:T(8,128)} pad(f32[4,1,256,1024]{3,2,1,0:T(8,128)} %convolution_bitcast_fusion.2, f32[]{:T(128)} %constant.6.clone.1), padding=0_0x1_0x0_0x0_0 | pad | bytes 12582916 | tf_op jit(solution)/shard_map/stack | solution.py:81
  72.8 9.2 %copy.15 = f32[2048,1024]{0,1:T(8,128)} copy(f32[2048,1024]{1,0:T(8,128)} %bitcast.193) | data formatting | bytes 16777216 | tf_op jit(solution)/shard_map/reshape;reshape | solution.py:46
  82.0 6.6 %stack.29.clone = f32[2,2,512,1024]{3,2,1,0:T(8,128)} pad(f32[2,1,512,1024]{3,2,1,0:T(8,128)} %convolution_bitcast_fusion.1, f32[]{:T(128)} %constant.6.clone.1), padding=0_0x1_0x0_0x0_0 | pad | bytes 12582916 | tf_op jit(solution)/shard_map/stack | solution.py:81
  88.5 9.2 %copy.18 = f32[2048,1024]{0,1:T(8,128)} copy(f32[2048,1024]{1,0:T(8,128)} %bitcast.194) | data formatting | bytes 16777216 | tf_op jit(solution)/shard_map/reshape;reshape | solution.py:46
  97.7 6.5 %stack.31 = f32[1,2,1024,1024]{3,2,1,0:T(8,128)} pad(f32[1,1,1024,1024]{3,2,1,0:T(8,128)} %convolution_bitcast_fusion, f32[]{:T(128)} %constant.6.clone.1), padding=0_0x1_0x0_0x0_0 | pad | bytes 12582916 | tf_op jit(solution)/shard_map/stack | solution.py:81
  104.3 9.2 %copy.19 = f32[2048,1024]{0,1:T(8,128)} copy(f32[2048,1024]{1,0:T(8,128)} %bitcast.191) | data formatting | bytes 16777216 | tf_op jit(solution)/shard_map/reshape;reshape | solution.py:46
  113.5 9.2 %copy.9 = f32[2048,1024]{0,1:T(8,128)} copy(f32[2048,1024]{1,0:T(8,128)} %bitcast.190) | data formatting | bytes 16777216 | tf_op jit(solution)/shard_map/reshape;reshape | solution.py:46
  122.7 1.3 fusion.22
  124.0 0.0 collective-permute-done.1
  124.0 0.1 add.42
  124.1 2.6 %collective-permute-start.2 = (bf16[128,1024]{1,0:T(8,128)(2,1)S(1)}, bf16[128,1024]{1,0:T(8,128)(2,1)}, u32[]{:S(2)}, u32[]{:S(2)}) collective-permute-start(bf16[128,1024]{1,0:T(8,128)(2,1)S(1)} %add.42), channel_id=1, source_target_pairs={{0,16},{4,20},{8,24},{12,28},{16,0},{20,4},{24,8},{28,12},{1,17},{... | collective-permute-start | bytes 786440 | tf_op jit(solution)/shard_map/ppermute | solution.py:12
  126.7 1.3 fusion.23
  128.0 10.9 %collective-permute-done.2 = bf16[128,1024]{1,0:T(8,128)(2,1)} collective-permute-done((bf16[128,1024]{1,0:T(8,128)(2,1)S(1)}, bf16[128,1024]{1,0:T(8,128)(2,1)}, u32[]{:S(2)}, u32[]{:S(2)}) %collective-permute-start.2) | collective-permute-done | bytes 262176 | tf_op jit(solution)/shard_map/ppermute | solution.py:12
  139.0 0.0 copy-start.1
  139.0 17.3 %fusion.1 = bf16[2048,1024]{0,1:T(8,128)(2,1)} fusion(f32[1024,2048]{1,0:T(8,128)S(1)} %fusion.23, f32[1024,2048]{1,0:T(8,128)S(1)} %fusion.22, f32[2048,1024]{0,1:T(8,128)} %copy.19, f32[2048,1024]{0,1:T(8,128)} %copy.18, f32[2048,1024]{0,1:T(8,128)} %copy.15, f32[2048,1024]{0,1:T(8,128)} %copy.12, f32[2048,1024]{0,1:T(8,128)} %copy.9, ...), kind=kOutput, calls=%fused_computation.2 | convolution fusion | flops 570556416 | bytes 64225280 | tf_op jit(solution)/shard_map/dot_general | solution.py:87
  156.3 6.4 %copy.20 = bf16[2048,1024]{1,0:T(8,128)(2,1)} copy(bf16[2048,1024]{0,1:T(8,128)(2,1)} %fusion.1) | data formatting | bytes 8388608 | tf_op jit(solution)/shard_map/convert_element_type | solution.py:89
  162.7 0.0 copy-done.1
  (2 shorter events, 0.1 us)
Async XLA Ops:
  0.0 20.7 %copy-start = (f32[16,8]{0,1:T(8,128)S(1)}, f32[16,8]{0,1:T(8,128)}, u32[]{:S(2)}) copy-start(f32[16,8]{0,1:T(8,128)} %param.9) | copy-start | bytes 1540
  12.0 31.9 %collective-permute-start = (f32[128,1024]{1,0:T(8,128)S(1)}, f32[128,1024]{1,0:T(8,128)S(1)}, u32[]{:S(2)}, u32[]{:S(2)}) collective-permute-start(f32[128,1024]{1,0:T(8,128)S(1)} %fusion.36), channel_id=1, source_target_pairs={{0,4},{4,0},{8,12},{12,8},{16,20},{20,16},{24,28},{28,24},{1,5},{5... | collective-permute-start | bytes 1572872 | tf_op jit(solution)/shard_map/ppermute | solution.py:12
  43.9 80.1 %collective-permute-start.1 = (f32[128,1024]{1,0:T(8,128)S(1)}, f32[128,1024]{1,0:T(8,128)S(1)}, u32[]{:S(2)}, u32[]{:S(2)}) collective-permute-start(f32[128,1024]{1,0:T(8,128)S(1)} %add.40), channel_id=1, source_target_pairs={{0,8},{4,12},{8,0},{12,4},{16,24},{20,28},{24,16},{28,20},{1,9},{5... | collective-permute-start | bytes 1572872 | tf_op jit(solution)/shard_map/ppermute | solution.py:12
  124.1 14.9 %collective-permute-start.2 = (bf16[128,1024]{1,0:T(8,128)(2,1)S(1)}, bf16[128,1024]{1,0:T(8,128)(2,1)}, u32[]{:S(2)}, u32[]{:S(2)}) collective-permute-start(bf16[128,1024]{1,0:T(8,128)(2,1)S(1)} %add.42), channel_id=1, source_target_pairs={{0,16},{4,20},{8,24},{12,28},{16,0},{20,4},{24,8},{28,12},{1,17},{... | collective-permute-start | bytes 786440 | tf_op jit(solution)/shard_map/ppermute | solution.py:12
  139.0 23.7 %copy-start.1 = (f32[16,8]{0,1:T(8,128)S(1)}, f32[16,8]{0,1:T(8,128)}, u32[]{:S(2)}) copy-start(f32[16,8]{0,1:T(8,128)} %param.9) | copy-start | bytes 1540
where the time goes:
time: 164 us; the launch traced here: 163 us
  local copies, waits for them, and re-layouts  79.5 us (48%)
  matrix products  49.9 us (30%)
  blocking collectives  16.2 us (10%)
  waiting for transfers between devices  10.9 us (7%)
  starting transfers between devices  5.84 us (4%)
    another operation x5, local copies, waits for them, and re-layouts, weigh(): part.reshape(tok_rows, head_count, head_width) * share[level][:, :, None]  46.1 us
    another operation x4, local copies, waits for them, and re-layouts, local(): jnp.stack([jnp.zeros_like(upper_half_branch), upper_half_branch], axis=1)  26.2 us
    dot_general x3, matrix products, local(): jnp.dot(q_whole, cumulative_memory, preferred_element_type=jnp.float32)  19.9 us
    dot_general x4, matrix products, local(): jnp.einsum('bsk,bkc->bsc', query_blocked[:, 1], cumulative_memory, prefer...  18.8 us
    ppermute x3, waiting for transfers between devices, swapped(): return lax.ppermute(value, axis, pairs)  10.9 us
    all_gather x1, blocking collectives, local(): lax.all_gather(keys, 'head', axis=0, tiled=True)  9 us
    all_gather x1, blocking collectives, local(): lax.all_gather(queries, 'head', axis=0, tiled=True)  7.22 us
    dot_general x1, matrix products, local(): jnp.einsum('nij,njc->nic', scores, values.reshape(groups, GROUP, columns)...  6.98 us
  transfers between devices with their start and end apart: 3, of which 1 were waited for; matrix products, arithmetic and copies ran while one was open for 63% of the time, Pallas kernels for 0%

commit v1 on v0

v1 whole, which is shorter than its diff:
```python
import functools

import jax
import jax.numpy as jnp
from jax import lax
from jax.experimental import pallas as pl
from jax.experimental.pallas import tpu as pltpu
from jax.sharding import PartitionSpec as P

GROUP = 128
F32 = jnp.float32
BF16 = jnp.bfloat16


def exchanged(value, axis, mask):
    pairs = [(source, source ^ mask) for source in range(lax.axis_size(axis))]
    return lax.ppermute(value, axis, pairs)


def dot(a, b):
    return jnp.dot(a, b, preferred_element_type=F32)


def place(pieces, me, target):
    rows = pieces[0].shape[0]
    for j, piece in enumerate(pieces):
        start = pl.multiple_of((me ^ j) * rows, rows)
        target[pl.ds(start, rows), :] = piece[...]


def state_kernel(count, place_ref, *refs):
    pieces, v_ref, s_ref, sb_ref, k_all, k_t = refs[:count], *refs[count:]

    @pl.when(pl.program_id(0) == 0)
    def _():
        place(pieces, place_ref[0], k_all)
        k_t[...] = k_all[...].T

    s = dot(k_t[...], v_ref[...])
    s_ref[...] = s
    sb_ref[...] = s.astype(BF16)


def shares(rows_ref, table_ref, head):
    rows = rows_ref[...]
    weights = jnp.zeros(rows.shape, F32)
    for c in range(table_ref.shape[0]):
        weights = jnp.where(rows == c, table_ref[c, head], weights)
    return weights / jnp.sum(weights, axis=0, keepdims=True)


def local_kernel(count, place_ref, table_ref, *refs):
    ks, qs = refs[:count], refs[count : 2 * count]
    v_ref, rows_ref, acc_ref, share_ref, q_all, k_all, k_t, sc = refs[2 * count :]
    tokens = q_all.shape[0]
    groups = tokens // GROUP

    @pl.when(pl.program_id(0) == 0)
    def _():
        place(ks, place_ref[0], k_all)
        place(qs, place_ref[0], q_all)
        k_t[...] = k_all[...].T
        row = lax.broadcasted_iota(jnp.int32, (GROUP, GROUP), 0)
        col = lax.broadcasted_iota(jnp.int32, (GROUP, GROUP), 1)
        for g in range(groups):
            at = slice(g * GROUP, (g + 1) * GROUP)
            own = dot(q_all[at, :], k_t[:, at])
            sc[at, GROUP:] = jnp.where(col <= row, own, 0.0)
            if g % 2 == 1:
                sc[at, :GROUP] = dot(q_all[at, :], k_t[:, (g - 1) * GROUP : g * GROUP])

    share = shares(rows_ref, table_ref, pl.program_id(0))
    share_ref[...] = share[None]
    share_t = share.T

    def scaled(value, at, level):
        return (value * share_t[at, level : level + 1]).astype(BF16)

    for g in range(groups):
        at = slice(g * GROUP, (g + 1) * GROUP)
        lhs = scaled(sc[at, GROUP:], at, 0)
        first = g
        if g % 2 == 1:
            lhs = jnp.concatenate([scaled(sc[at, :GROUP], at, 1), lhs], axis=1)
            first = g - 1
        acc_ref[at, :] = dot(lhs, v_ref[first * GROUP : (g + 1) * GROUP, :])
    pair = 2 * GROUP
    subtrees = [
        dot(k_t[:, p * pair : (p + 1) * pair], v_ref[p * pair : (p + 1) * pair, :])
        for p in range(groups // 2 - 1)
    ]
    half = pair
    level = 2
    while 2 * half <= tokens:
        for b in range(tokens // (2 * half)):
            at = slice((2 * b + 1) * half, (2 * b + 2) * half)
            left = subtrees[2 * b].astype(BF16)
            acc_ref[at, :] += dot(scaled(q_all[at, :].astype(F32), at, level), left)
        subtrees = [a + b for a, b in zip(subtrees[0::2], subtrees[1::2])]
        half *= 2
        level += 1


def far_kernel(count, bits, first_level, place_ref, *refs):
    qs = refs[:count]
    states = refs[count : count + bits]
    share_ref, acc_ref, out_ref, q_all = refs[count + bits :]

    @pl.when(pl.program_id(0) == 0)
    def _():
        place(qs, place_ref[0], q_all)

    share_t = share_ref[0].T
    q = q_all[...].astype(F32)
    parts = []
    for b in range(bits):
        on = (place_ref[1] >> b & 1).astype(F32)
        s = share_t[:, first_level + b : first_level + b + 1] * on
        parts.append((q * s).astype(BF16))
    lhs = jnp.concatenate(parts, axis=1)
    rhs = jnp.concatenate([s[...] for s in states], axis=0)
    out_ref[...] = (acc_ref[...] + dot(lhs, rhs)).astype(BF16)


def local(queries, keys, values, tier_weight_rows, level_table):
    tokens, columns = values.shape
    heads = level_table.shape[1]
    levels = tier_weight_rows.shape[0]
    width = columns // heads
    depth = keys.shape[1]
    rows = keys.shape[0]
    count = lax.axis_size("head")
    context_bits = lax.axis_size("ctx").bit_length() - 1
    local_bits = (tokens // GROUP).bit_length() - 1
    me = jnp.stack([lax.axis_index("head"), lax.axis_index("ctx")]).astype(jnp.int32)

    ks, qs = {0: keys}, {0: queries}
    bit = count // 2
    while bit:
        for held in (ks, qs):
            held.update({j | bit: exchanged(piece, "head", bit) for j, piece in held.items()})
        bit //= 2
    ks = [ks[j] for j in range(count)]
    qs = [qs[j] for j in range(count)]

    wide = min(columns, 2 * width)
    whole = pl.BlockSpec((rows, depth), lambda i, *_: (0, 0))
    column = pl.BlockSpec((tokens, width), lambda i, *_: (0, i))
    state_column = pl.BlockSpec((depth, width), lambda i, *_: (0, i))
    share_spec = pl.BlockSpec((1, levels, tokens), lambda i, *_: (i, 0, 0))
    params = pltpu.CompilerParams(
        dimension_semantics=("arbitrary",), vmem_limit_bytes=32 * 2**20
    )
    total, total_b = pl.pallas_call(
        functools.partial(state_kernel, count),
        out_shape=(
            jax.ShapeDtypeStruct((depth, columns), F32),
            jax.ShapeDtypeStruct((depth, columns), BF16),
        ),
        grid_spec=pltpu.PrefetchScalarGridSpec(
            num_scalar_prefetch=1,
            grid=(columns // wide,),
            in_specs=[whole] * count + [pl.BlockSpec((tokens, wide), lambda i, *_: (0, i))],
            out_specs=[pl.BlockSpec((depth, wide), lambda i, *_: (0, i))] * 2,
            scratch_shapes=[pltpu.VMEM((tokens, depth), BF16), pltpu.VMEM((depth, tokens), BF16)],
        ),
        compiler_params=params,
        name="state",
    )(me, *ks, values)

    states = []
    for b in range(context_bits):
        mask = 2 ** (b + 1) - 2 if b else 1
        incoming = exchanged(total_b, "ctx", mask)
        states.append(incoming)
        if b + 1 < context_bits:
            total = total + incoming.astype(F32)
            total_b = total.astype(BF16)

    acc, share = pl.pallas_call(
        functools.partial(local_kernel, count),
        out_shape=(
            jax.ShapeDtypeStruct((tokens, columns), F32),
            jax.ShapeDtypeStruct((heads, levels, tokens), F32),
        ),
        grid_spec=pltpu.PrefetchScalarGridSpec(
            num_scalar_prefetch=2,
            grid=(heads,),
            in_specs=[whole] * (2 * count)
            + [column, pl.BlockSpec((levels, tokens), lambda i, *_: (0, 0))],
            out_specs=[column, share_spec],
            scratch_shapes=[
                pltpu.VMEM((tokens, depth), BF16),
                pltpu.VMEM((tokens, depth), BF16),
                pltpu.VMEM((depth, tokens), BF16),
                pltpu.VMEM((tokens, 2 * GROUP), F32),
            ],
        ),
        compiler_params=params,
        cost_estimate=pl.CostEstimate(
            flops=8 * tokens * depth * columns, transcendentals=0, bytes_accessed=14 * tokens * columns
        ),
        name="near",
    )(me, level_table, *ks, *qs, values, tier_weight_rows)

    return pl.pallas_call(
        functools.partial(far_kernel, count, context_bits, 1 + local_bits),
        out_shape=jax.ShapeDtypeStruct((tokens, columns), BF16),
        grid_spec=pltpu.PrefetchScalarGridSpec(
            num_scalar_prefetch=1,
            grid=(heads,),
            in_specs=[whole] * count + [state_column] * context_bits + [share_spec, column],
            out_specs=column,
            scratch_shapes=[pltpu.VMEM((tokens, depth), BF16)],
        ),
        compiler_params=params,
        name="far",
    )(me, *qs, *states, share, acc)


def solution(mesh):
    placed = (
        P(("ctx", "head"), None),
        P(("ctx", "head"), None),
        P("ctx", "head"),
        P(None, "ctx"),
        P(None, "head"),
    )
    return jax.shard_map(
        local, mesh=mesh, in_specs=placed, out_specs=P("ctx", "head"), check_vma=False
    )
```

time: 164 us -> 65.4 us (0.40)
  local copies, waits for them, and re-layouts: 79.5 us -> 5.36 us
  matrix products: 49.9 us -> 0 us
  Pallas kernels: 0 us -> 31.7 us
  blocking collectives: 16.2 us -> 0 us
  starting transfers between devices: 5.84 us -> 12 us
  waiting for transfers between devices: 10.9 us -> 15.9 us
    another operation x9 -> x0, local copies, waits for them, and re-layouts: 72.3 us -> none  [the longest x5 46.1 us: weigh(): part.reshape(tok_rows, head_count, head_width) * share[level][:, :, None]]
    dot_general x10 -> x0, matrix products: 49.9 us -> none  [the longest x3 19.9 us: local(): jnp.dot(q_whole, cumulative_memory, preferred_element_type=jnp.float32)]
    pallas_call x0 -> x3, Pallas kernels: none -> 31.7 us  [the longest x1 14.7 us: local(): pl.pallas_call(functools.partial(local_kernel, count), out_shape=(jax.Sha...]
    all_gather x2 -> x0, blocking collectives: 16.2 us -> none  [the longest x1 9 us: local(): lax.all_gather(keys, 'head', axis=0, tiled=True)]
    convert_element_type x1 -> x0, local copies, waits for them, and re-layouts: 6.4 us -> none  [local(): return total.astype(jnp.bfloat16)]
    ppermute x3 -> x9, starting transfers between devices: 5.84 us -> 12 us  [exchanged(): return lax.ppermute(value, axis, pairs)]
    unnamed x4 -> x15, local copies, waits for them, and re-layouts: 0.01 us -> 5.36 us
    ppermute x3 -> x9, waiting for transfers between devices: 10.9 us -> 15.9 us  [exchanged(): return lax.ppermute(value, axis, pairs)]
  transfers between devices with their start and end apart: 3 -> 9, of which waited for: 1 -> 5; matrix products, arithmetic and copies ran while one was open for 63% -> 0% of each run, Pallas kernels for 0% -> 23%
where the time goes in v1:
time: 65.4 us; the launch traced here: 65.2 us
  Pallas kernels  31.7 us (48%)
  waiting for transfers between devices  15.9 us (24%)
  starting transfers between devices  12 us (18%)
  local copies, waits for them, and re-layouts  5.36 us (8%)
    ppermute x9, waiting for transfers between devices, exchanged(): return lax.ppermute(value, axis, pairs)  15.9 us
    pallas_call x1, Pallas kernels, local(): pl.pallas_call(functools.partial(local_kernel, count), out_shape=(jax.Sha...  14.7 us
    pallas_call x1, Pallas kernels, local(): pl.pallas_call(functools.partial(far_kernel, count, context_bits, 1 + loc...  14.3 us
    ppermute x9, starting transfers between devices, exchanged(): return lax.ppermute(value, axis, pairs)  12 us
    unnamed x15, local copies, waits for them, and re-layouts  5.36 us
    pallas_call x1, Pallas kernels, local(): pl.pallas_call(functools.partial(state_kernel, count), out_shape=(jax.Sha...  2.71 us
  transfers between devices with their start and end apart: 9, of which 5 were waited for; matrix products, arithmetic and copies ran while one was open for 0% of the time, Pallas kernels for 23%

profile of v1, /device:TPU:0, one launch (start us, length us, event | category | flops | bytes accessed | tf_op | source)
XLA Modules:
  0.0 65.2 jit_solution(12663470809094213717)
XLA Ops:
  0.0 0.0 copy-start.6
  0.0 3.0 %collective-permute-start.4 = (bf16[512,128]{1,0:T(8,128)(2,1)}, bf16[512,128]{1,0:T(8,128)(2,1)S(1)}, u32[]{:S(2)}, u32[]{:S(2)}) collective-permute-start(bf16[512,128]{1,0:T(8,128)(2,1)} %refs_0_.4), channel_id=1, source_target_pairs={{0,2},{1,3},{2,0},{3,1},{4,6},{5,7},{6,4},{7,5},{8,10},{9,11},{10,... | collective-permute-start | bytes 393224 | tf_op jit(solution)/shard_map/ppermute | solution.py:17
  3.0 0.0 collective-permute-start.3
  3.0 3.7 %collective-permute-done.4.refs_2_ = bf16[512,128]{1,0:T(8,128)(2,1)S(1)} collective-permute-done((bf16[512,128]{1,0:T(8,128)(2,1)}, bf16[512,128]{1,0:T(8,128)(2,1)S(1)}, u32[]{:S(2)}, u32[]{:S(2)}) %collective-permute-start.4) | collective-permute-done | bytes 131104 | tf_op jit(solution)/shard_map/ppermute | solution.py:17
  6.7 0.0 collective-permute-start.5
  6.7 0.1 pad_add_fusion.place_ref
  6.8 0.0 collective-permute-done.3.refs_1_
  6.8 1.3 %collective-permute-done.5.refs_3_ = bf16[512,128]{1,0:T(8,128)(2,1)S(1)} collective-permute-done((bf16[512,128]{1,0:T(8,128)(2,1)S(1)}, bf16[512,128]{1,0:T(8,128)(2,1)S(1)}, u32[]{:S(2)}, u32[]{:S(2)}) %collective-permute-start.5) | collective-permute-done | bytes 131104 | tf_op jit(solution)/shard_map/ppermute | solution.py:17
  8.1 0.0 copy-start
  8.1 2.2 %copy-done = bf16[2048,1024]{1,0:T(8,128)(2,1)S(1)} copy-done((bf16[2048,1024]{1,0:T(8,128)(2,1)S(1)}, bf16[2048,1024]{1,0:T(8,128)(2,1)}, u32[]{:S(2)}) %copy-start) | copy-done | bytes 4194328
  10.2 0.0 copy-start.3
  10.2 0.9 %copy-done.3 = bf16[512,128]{1,0:T(8,128)(2,1)S(1)} copy-done((bf16[512,128]{1,0:T(8,128)(2,1)S(1)}, bf16[512,128]{1,0:T(8,128)(2,1)}, u32[]{:S(2)}) %copy-start.3) | copy-done | bytes 131096
  11.1 0.0 copy-start.2
  11.1 0.0 copy-start.4
  11.1 0.0 copy-start.5
  11.2 2.7 %state.1 = (f32[128,1024]{1,0:T(8,128)S(1)}, bf16[128,1024]{1,0:T(8,128)(2,1)S(1)}) custom-call(s32[2]{0:T(128)S(1)} %pad_add_fusion.place_ref, bf16[512,128]{1,0:T(8,128)(2,1)S(1)} %copy-done.3, bf16[512,128]{1,0:T(8,128)(2,1)S(1)} %collective-permute-done.3.refs_1_, bf16[512,128]{1,0:T(8,128)(2,1)S(1)} %collective-permute-done.4.refs_2_, ...), custom_call_target="tpu_custom_call" | custom-call | tf_op jit(solution)/shard_map/state/pallas_call | solution.py:154
  13.9 1.8 %collective-permute-start.6 = (bf16[128,1024]{1,0:T(8,128)(2,1)S(1)}, bf16[128,1024]{1,0:T(8,128)(2,1)S(1)}, u32[]{:S(2)}, u32[]{:S(2)}) collective-permute-start(bf16[128,1024]{1,0:T(8,128)(2,1)S(1)} %get-tuple-element.9), channel_id=1, source_target_pairs={{0,4},{4,0},{8,12},{12,8},{16,20},{20,16},{24,28},{28,24},{1,5},{5... | collective-permute-start | bytes 786440 | tf_op jit(solution)/shard_map/ppermute | solution.py:17
  15.7 6.6 %collective-permute-done.6.refs_4_ = bf16[128,1024]{1,0:T(8,128)(2,1)S(1)} collective-permute-done((bf16[128,1024]{1,0:T(8,128)(2,1)S(1)}, bf16[128,1024]{1,0:T(8,128)(2,1)S(1)}, u32[]{:S(2)}, u32[]{:S(2)}) %collective-permute-start.6) | collective-permute-done | bytes 262176 | tf_op jit(solution)/shard_map/ppermute | solution.py:17
  22.3 0.1 fusion
  22.4 1.9 %collective-permute-start.7 = (bf16[128,1024]{1,0:T(8,128)(2,1)S(1)}, bf16[128,1024]{1,0:T(8,128)(2,1)S(1)}, u32[]{:S(2)}, u32[]{:S(2)}) collective-permute-start(bf16[128,1024]{1,0:T(8,128)(2,1)S(1)} %fusion), channel_id=1, source_target_pairs={{0,8},{4,12},{8,0},{12,4},{16,24},{20,28},{24,16},{28,20},{1,9},{5... | collective-permute-start | bytes 786440 | tf_op jit(solution)/shard_map/ppermute | solution.py:17
  24.2 0.0 copy-done.2
  24.2 1.5 %collective-permute-start.1 = (bf16[512,128]{1,0:T(8,128)(2,1)S(1)}, bf16[512,128]{1,0:T(8,128)(2,1)S(1)}, u32[]{:S(2)}, u32[]{:S(2)}) collective-permute-start(bf16[512,128]{1,0:T(8,128)(2,1)S(1)} %copy-done.2), channel_id=1, source_target_pairs={{0,2},{1,3},{2,0},{3,1},{4,6},{5,7},{6,4},{7,5},{8,10},{9,11},{10,... | collective-permute-start | bytes 393224 | tf_op jit(solution)/shard_map/ppermute | solution.py:17
  25.8 0.0 collective-permute-start
  25.8 3.4 %collective-permute-done.1.refs_6_.refs_2_ = bf16[512,128]{1,0:T(8,128)(2,1)S(1)} collective-permute-done((bf16[512,128]{1,0:T(8,128)(2,1)S(1)}, bf16[512,128]{1,0:T(8,128)(2,1)S(1)}, u32[]{:S(2)}, u32[]{:S(2)}) %collective-permute-start.1) | collective-permute-done | bytes 131104 | tf_op jit(solution)/shard_map/ppermute | solution.py:17
  29.2 0.0 collective-permute-start.2
  29.2 0.8 %collective-permute-done.7.refs_5_ = bf16[128,1024]{1,0:T(8,128)(2,1)S(1)} collective-permute-done((bf16[128,1024]{1,0:T(8,128)(2,1)S(1)}, bf16[128,1024]{1,0:T(8,128)(2,1)S(1)}, u32[]{:S(2)}, u32[]{:S(2)}) %collective-permute-start.7) | collective-permute-done | bytes 262176 | tf_op jit(solution)/shard_map/ppermute | solution.py:17
  30.0 0.1 add_convert_fusion
  30.1 3.8 %collective-permute-start.8 = (bf16[128,1024]{1,0:T(8,128)(2,1)S(1)}, bf16[128,1024]{1,0:T(8,128)(2,1)S(1)}, u32[]{:S(2)}, u32[]{:S(2)}) collective-permute-start(bf16[128,1024]{1,0:T(8,128)(2,1)S(1)} %add_convert_fusion), channel_id=1, source_target_pairs={{0,24},{4,28},{8,16},{12,20},{16,8},{20,12},{24,0},{28,4},{1,25},{... | collective-permute-start | bytes 786440 | tf_op jit(solution)/shard_map/ppermute | solution.py:17
  33.9 0.0 copy-done.6
  33.9 0.1 copy.6.table_ref
  34.0 0.0 collective-permute-done.refs_5_.refs_1_
  34.0 0.0 collective-permute-done.2.refs_7_.refs_3_
  34.0 0.0 copy-done.4
  34.0 0.0 copy-done.5
  34.0 0.0 copy-start.1
  34.0 2.2 %copy-done.1 = bf16[2048,1024]{1,0:T(8,128)(2,1)S(1)} copy-done((bf16[2048,1024]{1,0:T(8,128)(2,1)S(1)}, bf16[2048,1024]{1,0:T(8,128)(2,1)}, u32[]{:S(2)}) %copy-start.1) | copy-done | bytes 4194328
  36.2 14.7 %near.1 = (f32[2048,1024]{1,0:T(8,128)S(1)}, f32[8,8,2048]{2,1,0:T(8,128)S(1)}) custom-call(s32[2]{0:T(128)S(1)} %pad_add_fusion.place_ref, f32[16,8]{1,0:T(8,128)S(1)} %copy.6.table_ref, bf16[512,128]{1,0:T(8,128)(2,1)S(1)} %copy-done.4, bf16[512,128]{1,0:T(8,128)(2,1)S(1)} %collective-permute-done.3.refs_1_, ...), custom_call_target="tpu_custom_call" | custom-call | flops 2147483648 | bytes 29360128 | tf_op jit(solution)/shard_map/near/pallas_call | solution.py:180
  51.0 0.0 collective-permute-done.8.refs_6_
  51.0 14.3 %far.1 = bf16[2048,1024]{1,0:T(8,128)(2,1)} custom-call(s32[2]{0:T(128)S(1)} %pad_add_fusion.place_ref, bf16[512,128]{1,0:T(8,128)(2,1)S(1)} %copy-done.2, bf16[512,128]{1,0:T(8,128)(2,1)S(1)} %collective-permute-done.refs_5_.refs_1_, bf16[512,128]{1,0:T(8,128)(2,1)S(1)} %collective-permute-done.1.refs_6_.refs_2_, ...), custom_call_target="tpu_custom_call" | custom-call | tf_op jit(solution)/shard_map/far/pallas_call | solution.py:206
Async XLA Ops:
  0.0 33.9 %copy-start.6 = (f32[16,8]{0,1:T(8,128)S(1)}, f32[16,8]{0,1:T(8,128)}, u32[]{:S(2)}) copy-start(f32[16,8]{0,1:T(8,128)} %param.9) | copy-start | bytes 1540
  0.0 6.7 %collective-permute-start.4 = (bf16[512,128]{1,0:T(8,128)(2,1)}, bf16[512,128]{1,0:T(8,128)(2,1)S(1)}, u32[]{:S(2)}, u32[]{:S(2)}) collective-permute-start(bf16[512,128]{1,0:T(8,128)(2,1)} %refs_0_.4), channel_id=1, source_target_pairs={{0,2},{1,3},{2,0},{3,1},{4,6},{5,7},{6,4},{7,5},{8,10},{9,11},{10,... | collective-permute-start | bytes 393224 | tf_op jit(solution)/shard_map/ppermute | solution.py:17
  3.0 3.8 %collective-permute-start.3 = (bf16[512,128]{1,0:T(8,128)(2,1)}, bf16[512,128]{1,0:T(8,128)(2,1)S(1)}, u32[]{:S(2)}, u32[]{:S(2)}) collective-permute-start(bf16[512,128]{1,0:T(8,128)(2,1)} %refs_0_.4), channel_id=1, source_target_pairs={{0,1},{1,0},{2,3},{3,2},{4,5},{5,4},{6,7},{7,6},{8,9},{9,8},{10,11... | collective-permute-start | bytes 393224 | tf_op jit(solution)/shard_map/ppermute | solution.py:17
  6.7 1.3 %collective-permute-start.5 = (bf16[512,128]{1,0:T(8,128)(2,1)S(1)}, bf16[512,128]{1,0:T(8,128)(2,1)S(1)}, u32[]{:S(2)}, u32[]{:S(2)}) collective-permute-start(bf16[512,128]{1,0:T(8,128)(2,1)S(1)} %collective-permute-done.4.refs_2_), channel_id=1, source_target_pairs={{0,1},{1,0},{2,3},{3,2},{4,5},{5,4},{6,7},{7,6},{8,9},{9,8},{10,11... | collective-permute-start | bytes 393224 | tf_op jit(solution)/shard_map/ppermute | solution.py:17
  8.1 2.2 %copy-start = (bf16[2048,1024]{1,0:T(8,128)(2,1)S(1)}, bf16[2048,1024]{1,0:T(8,128)(2,1)}, u32[]{:S(2)}) copy-start(bf16[2048,1024]{1,0:T(8,128)(2,1)} %refs_8_.1) | copy-start | bytes 12582916
  10.2 0.9 %copy-start.3 = (bf16[512,128]{1,0:T(8,128)(2,1)S(1)}, bf16[512,128]{1,0:T(8,128)(2,1)}, u32[]{:S(2)}) copy-start(bf16[512,128]{1,0:T(8,128)(2,1)} %refs_0_.4) | copy-start | bytes 393220
  11.1 13.1 %copy-start.2 = (bf16[512,128]{1,0:T(8,128)(2,1)S(1)}, bf16[512,128]{1,0:T(8,128)(2,1)}, u32[]{:S(2)}) copy-start(bf16[512,128]{1,0:T(8,128)(2,1)} %refs_0_.5) | copy-start | bytes 393220
  11.1 22.9 %copy-start.4 = (bf16[512,128]{1,0:T(8,128)(2,1)S(1)}, bf16[512,128]{1,0:T(8,128)(2,1)}, u32[]{:S(2)}) copy-start(bf16[512,128]{1,0:T(8,128)(2,1)} %refs_0_.4) | copy-start | bytes 393220
  11.1 22.9 %copy-start.5 = (s32[8,2048]{1,0:T(8,128)S(1)}, s32[8,2048]{1,0:T(8,128)}, u32[]{:S(2)}) copy-start(s32[8,2048]{1,0:T(8,128)} %refs_9_.1) | copy-start | bytes 196612
  13.9 8.4 %collective-permute-start.6 = (bf16[128,1024]{1,0:T(8,128)(2,1)S(1)}, bf16[128,1024]{1,0:T(8,128)(2,1)S(1)}, u32[]{:S(2)}, u32[]{:S(2)}) collective-permute-start(bf16[128,1024]{1,0:T(8,128)(2,1)S(1)} %get-tuple-element.9), channel_id=1, source_target_pairs={{0,4},{4,0},{8,12},{12,8},{16,20},{20,16},{24,28},{28,24},{1,5},{5... | collective-permute-start | bytes 786440 | tf_op jit(solution)/shard_map/ppermute | solution.py:17
  22.4 7.6 %collective-permute-start.7 = (bf16[128,1024]{1,0:T(8,128)(2,1)S(1)}, bf16[128,1024]{1,0:T(8,128)(2,1)S(1)}, u32[]{:S(2)}, u32[]{:S(2)}) collective-permute-start(bf16[128,1024]{1,0:T(8,128)(2,1)S(1)} %fusion), channel_id=1, source_target_pairs={{0,8},{4,12},{8,0},{12,4},{16,24},{20,28},{24,16},{28,20},{1,9},{5... | collective-permute-start | bytes 786440 | tf_op jit(solution)/shard_map/ppermute | solution.py:17
  24.2 5.0 %collective-permute-start.1 = (bf16[512,128]{1,0:T(8,128)(2,1)S(1)}, bf16[512,128]{1,0:T(8,128)(2,1)S(1)}, u32[]{:S(2)}, u32[]{:S(2)}) collective-permute-start(bf16[512,128]{1,0:T(8,128)(2,1)S(1)} %copy-done.2), channel_id=1, source_target_pairs={{0,2},{1,3},{2,0},{3,1},{4,6},{5,7},{6,4},{7,5},{8,10},{9,11},{10,... | collective-permute-start | bytes 393224 | tf_op jit(solution)/shard_map/ppermute | solution.py:17
  25.8 8.3 %collective-permute-start = (bf16[512,128]{1,0:T(8,128)(2,1)S(1)}, bf16[512,128]{1,0:T(8,128)(2,1)S(1)}, u32[]{:S(2)}, u32[]{:S(2)}) collective-permute-start(bf16[512,128]{1,0:T(8,128)(2,1)S(1)} %copy-done.2), channel_id=1, source_target_pairs={{0,1},{1,0},{2,3},{3,2},{4,5},{5,4},{6,7},{7,6},{8,9},{9,8},{10,11... | collective-permute-start | bytes 393224 | tf_op jit(solution)/shard_map/ppermute | solution.py:17
  29.2 4.8 %collective-permute-start.2 = (bf16[512,128]{1,0:T(8,128)(2,1)S(1)}, bf16[512,128]{1,0:T(8,128)(2,1)S(1)}, u32[]{:S(2)}, u32[]{:S(2)}) collective-permute-start(bf16[512,128]{1,0:T(8,128)(2,1)S(1)} %collective-permute-done.1.refs_6_.refs_2_), channel_id=1, source_target_pairs={{0,1},{1,0},{2,3},{3,2},{4,5},{5,4},{6,7},{7,6},{8,9},{9,8},{10,11... | collective-permute-start | bytes 393224 | tf_op jit(solution)/shard_map/ppermute | solution.py:17
  30.1 20.9 %collective-permute-start.8 = (bf16[128,1024]{1,0:T(8,128)(2,1)S(1)}, bf16[128,1024]{1,0:T(8,128)(2,1)S(1)}, u32[]{:S(2)}, u32[]{:S(2)}) collective-permute-start(bf16[128,1024]{1,0:T(8,128)(2,1)S(1)} %add_convert_fusion), channel_id=1, source_target_pairs={{0,24},{4,28},{8,16},{12,20},{16,8},{20,12},{24,0},{28,4},{1,25},{... | collective-permute-start | bytes 786440 | tf_op jit(solution)/shard_map/ppermute | solution.py:17
  34.0 2.2 %copy-start.1 = (bf16[2048,1024]{1,0:T(8,128)(2,1)S(1)}, bf16[2048,1024]{1,0:T(8,128)(2,1)}, u32[]{:S(2)}) copy-start(bf16[2048,1024]{1,0:T(8,128)(2,1)} %refs_8_.1) | copy-start | bytes 12582916

commit v2 on v0

v2 whole, which is shorter than its diff:
```python
import functools

import jax
import jax.numpy as jnp
from jax import lax
from jax.experimental import pallas as pl
from jax.experimental.pallas import tpu as pltpu
from jax.sharding import PartitionSpec as P


GROUP = 128
LANES = 128
F32 = jnp.float32
BF16 = jnp.bfloat16
VMEM = pl.BlockSpec(memory_space=pltpu.VMEM)
SMEM = pl.BlockSpec(memory_space=pltpu.SMEM)
HBM = pl.BlockSpec(memory_space=pltpu.HBM)


def exchanged(value, axis, mask):
    pairs = [(source, source ^ mask) for source in range(lax.axis_size(axis))]
    return lax.ppermute(value, axis, pairs)


def dot(a, b):
    return jnp.dot(a, b, preferred_element_type=F32)


def piece_rows(me, j, rows):
    return pl.ds(pl.multiple_of((me ^ j) * rows, rows), rows)


def split_shares(rows_ref, table_ref, heads):
    rows = rows_ref[...]
    levels, tokens = rows.shape
    hits = [rows == c for c in range(table_ref.shape[0])]
    found = []
    for head in range(heads):
        weights = jnp.zeros(rows.shape, F32)
        for c, hit in enumerate(hits):
            weights = jnp.where(hit, table_ref[c, head], weights)
        found.append(weights / jnp.sum(weights, axis=0, keepdims=True))
    share = jnp.concatenate(found, axis=0)
    high = share.astype(BF16).astype(F32)
    low = share - high
    spare = -2 * heads * levels % LANES
    parts = [high, low]
    if spare:
        parts.append(jnp.zeros((spare, tokens), F32))
    return jnp.concatenate(parts, axis=0).astype(BF16)


def early_kernel(early, heads, me_ref, table_ref, *refs):
    ks = refs[: early - 1]
    rows_hbm, q_hbm, k_hbm, v_hbm, q_out, k_out, v_out, s_ref, share_ref, rows_ref, sems = refs[
        early - 1 :
    ]
    me = me_ref[0]
    rows = k_out.shape[0]
    count = v_out.shape[0] // rows
    small = [
        pltpu.make_async_copy(source, target, sems.at[count + n])
        for n, (source, target) in enumerate(
            ((rows_hbm, rows_ref), (k_hbm, k_out), (q_hbm, q_out))
        )
    ]
    copies = []
    for j in range(count):
        at = piece_rows(me, j, rows)
        copies.append(pltpu.make_async_copy(v_hbm.at[at, :], v_out.at[at, :], sems.at[j]))
    for copy in small + copies:
        copy.start()
    small[0].wait()
    share_ref[...] = split_shares(rows_ref, table_ref, heads).T
    small[1].wait()
    small[2].wait()
    for j in range(early):
        copies[j].wait()
        k = ks[j - 1] if j else k_out
        part = dot(k[...].T, v_out[piece_rows(me, j, rows), :])
        s_ref[...] = part if j == 0 else s_ref[...] + part
    for j in range(early, count):
        copies[j].wait()


def state_kernel(which, me_ref, *refs):
    ks = refs[: len(which)]
    v_ref, before_ref, s_ref, b_ref = refs[len(which) :]
    rows = ks[0].shape[0]
    s = before_ref[...]
    for j, k in zip(which, ks):
        s = s + dot(k[...].T, v_ref[piece_rows(me_ref[0], j, rows), :])
    s_ref[...] = s
    b_ref[...] = s.astype(BF16)


def chooser(kinds, heads, levels, chunk, wide, level):
    row = lax.broadcasted_iota(jnp.int32, (kinds, wide), 0)
    col = lax.broadcasted_iota(jnp.int32, (kinds, wide), 1)
    width = wide // chunk[1]
    target = (chunk[0] * chunk[1] + col // width) * levels + level
    hit = (row == target) | (row == target + heads * levels)
    return jnp.where(hit, 1.0, 0.0).astype(BF16)


def local_kernel(count, heads, levels, me_ref, *refs):
    ks, qs = refs[:count], refs[count : 2 * count]
    v_ref, share_ref, acc_ref, q_all, k_t, sc = refs[2 * count :]
    tokens, columns = v_ref.shape
    groups = tokens // GROUP
    rows = ks[0].shape[0]
    width = columns // heads
    span = 2 if heads % 2 == 0 else 1
    wide = span * width
    kinds = share_ref.shape[1]
    me = me_ref[0]
    for j in range(count):
        q_all[piece_rows(me, j, rows), :] = qs[j][...]
        k_t[:, piece_rows(me, j, rows)] = ks[j][...].T
    row = lax.broadcasted_iota(jnp.int32, (GROUP, GROUP), 0)
    col = lax.broadcasted_iota(jnp.int32, (GROUP, GROUP), 1)
    for g in range(groups):
        at = slice(g * GROUP, (g + 1) * GROUP)
        own = dot(q_all[at, :], k_t[:, at])
        sc[at, GROUP:] = jnp.where(col <= row, own, 0.0).astype(BF16)
        if g % 2 == 1:
            before = slice((g - 1) * GROUP, g * GROUP)
            sc[at, :GROUP] = dot(q_all[at, :], k_t[:, before]).astype(BF16)

    @pl.loop(0, columns // wide)
    def _(i):
        cs = pl.ds(pl.multiple_of(i * wide, wide), wide)

        def choose(level):
            return chooser(kinds, heads, levels, (i, span), wide, level)

        own_level, pair_level = choose(0), choose(1)
        for g in range(groups):
            at = slice(g * GROUP, (g + 1) * GROUP)
            part = dot(share_ref[at, :], own_level) * dot(sc[at, GROUP:], v_ref[at, cs])
            if g % 2 == 1:
                before = slice((g - 1) * GROUP, g * GROUP)
                part = part + dot(share_ref[at, :], pair_level) * dot(
                    sc[at, :GROUP], v_ref[before, cs]
                )
            acc_ref[at, cs] = part
        pair = 2 * GROUP
        subtrees = [
            dot(k_t[:, p * pair : (p + 1) * pair], v_ref[p * pair : (p + 1) * pair, cs])
            for p in range(groups // 2 - 1)
        ]
        half = pair
        level = 2
        while 2 * half <= tokens:
            chosen = choose(level)
            step = min(half, 512)
            for b in range(tokens // (2 * half)):
                left = subtrees[2 * b].astype(BF16)
                for first in range((2 * b + 1) * half, (2 * b + 2) * half, step):
                    at = slice(first, first + step)
                    acc_ref[at, cs] += dot(share_ref[at, :], chosen) * dot(q_all[at, :], left)
            subtrees = [a + b for a, b in zip(subtrees[0::2], subtrees[1::2])]
            half *= 2
            level += 1


def far_parts(heads, levels, level, bit, me_ref, q_ref, share_ref, state_ref, i, wide, span):
    on = (me_ref[1] >> bit & 1) == 1
    chosen = chooser(share_ref.shape[1], heads, levels, (i, span), wide, level)
    chosen = jnp.where(on, chosen, jnp.zeros_like(chosen))
    cs = pl.ds(pl.multiple_of(i * wide, wide), wide)
    state = state_ref[:, cs]
    tokens = q_ref.shape[0]
    step = min(tokens, 512)
    for first in range(0, tokens, step):
        at = slice(first, first + step)
        yield at, cs, dot(share_ref[at, :], chosen) * dot(q_ref[at, :], state)


def spans(heads, columns):
    span = 2 if heads % 2 == 0 else 1
    return span, span * columns // heads


def middle_kernel(heads, levels, level, bit, me_ref, q_ref, share_ref, state_ref, acc_ref, out_ref):
    span, wide = spans(heads, state_ref.shape[1])

    @pl.loop(0, heads // span)
    def _(i):
        for at, cs, part in far_parts(
            heads, levels, level, bit, me_ref, q_ref, share_ref, state_ref, i, wide, span
        ):
            out_ref[at, cs] = acc_ref[at, cs] + part


def last_kernel(
    heads, levels, level, bit, me_ref, q_ref, share_ref, state_ref, acc_ref, out_ref, buf, sems
):
    span, wide = spans(heads, state_ref.shape[1])
    copies = []
    for i in range(heads // span):
        for at, cs, part in far_parts(
            heads, levels, level, bit, me_ref, q_ref, share_ref, state_ref, i, wide, span
        ):
            at_cols = slice(i * wide, (i + 1) * wide)
            buf[at, at_cols] = (acc_ref[at, at_cols] + part).astype(BF16)
        cols = pl.ds(i * wide, wide)
        copies.append(pltpu.make_async_copy(buf.at[:, cols], out_ref.at[:, cols], sems.at[i]))
        copies[-1].start()
    for copy in copies:
        copy.wait()


def layer(queries, keys, values, tier_weight_rows, level_table):
    tokens, columns = values.shape
    heads = level_table.shape[1]
    levels = tier_weight_rows.shape[0]
    depth = keys.shape[1]
    rows = keys.shape[0]
    count = lax.axis_size("head")
    context_bits = lax.axis_size("ctx").bit_length() - 1
    local_bits = (tokens // GROUP).bit_length() - 1
    kinds = pl.cdiv(2 * heads * levels, LANES) * LANES
    me = jnp.stack([lax.axis_index("head"), lax.axis_index("ctx")]).astype(jnp.int32)

    ks, qs = {0: keys}, {0: queries}
    bit = count // 2
    while bit:
        for held in (ks, qs):
            for j, piece in list(held.items()):
                held[j | bit] = exchanged(piece, "head", bit)
        bit //= 2
    ks = [ks[j] for j in range(count)]
    qs = [qs[j] for j in range(count)]

    def shape(*dims, dtype=F32):
        return jax.ShapeDtypeStruct(dims, dtype)

    def cost(flops):
        return pl.CostEstimate(
            flops=flops * tokens * depth * columns, transcendentals=0, bytes_accessed=2 * tokens * columns
        )

    params = pltpu.CompilerParams(vmem_limit_bytes=24 * 2**20)
    early = max(1, count // 2)
    fixed = [
        pltpu.with_memory_space_constraint(a, pltpu.HBM)
        for a in (tier_weight_rows, queries, keys, values)
    ]
    qs[0], ks[0], held, total, share = pl.pallas_call(
        functools.partial(early_kernel, early, heads),
        out_shape=(
            shape(rows, depth, dtype=BF16),
            shape(rows, depth, dtype=BF16),
            shape(tokens, columns, dtype=BF16),
            shape(depth, columns),
            shape(tokens, kinds, dtype=BF16),
        ),
        in_specs=[SMEM, SMEM] + [VMEM] * (early - 1) + [HBM] * 4,
        out_specs=(VMEM,) * 5,
        scratch_shapes=[
            pltpu.VMEM((levels, tokens), jnp.int32),
            pltpu.SemaphoreType.DMA((count + 3,)),
        ],
        compiler_params=params,
        cost_estimate=cost(1),
        name="early",
    )(me, level_table, *ks[1:early], *fixed)

    total_b = total.astype(BF16)
    for which in (range(early, count - 1), range(count - 1, count)):
        which = [j for j in which if j >= early]
        if not which:
            continue
        total, total_b = pl.pallas_call(
            functools.partial(state_kernel, which),
            out_shape=(shape(depth, columns), shape(depth, columns, dtype=BF16)),
            in_specs=[SMEM] + [VMEM] * (len(which) + 2),
            out_specs=(VMEM, VMEM),
            compiler_params=params,
            name="state",
        )(me, *[ks[j] for j in which], held, total)

    states = []
    for b in range(context_bits):
        mask = 2 ** (b + 1) - 2 if b else 1
        incoming = exchanged(total_b, "ctx", mask)
        states.append(incoming)
        if b + 1 < context_bits:
            total = total + incoming.astype(F32)
            total_b = total.astype(BF16)

    acc, q_all = pl.pallas_call(
        functools.partial(local_kernel, count, heads, levels),
        out_shape=(shape(tokens, columns), shape(tokens, depth, dtype=BF16)),
        in_specs=[SMEM] + [VMEM] * (2 * count + 2),
        out_specs=(VMEM, VMEM),
        scratch_shapes=[pltpu.VMEM((depth, tokens), BF16), pltpu.VMEM((tokens, 2 * GROUP), BF16)],
        compiler_params=params,
        cost_estimate=cost(4),
        name="near",
    )(me, *ks, *qs, held, share)

    for b in range(context_bits - 1):
        acc = pl.pallas_call(
            functools.partial(middle_kernel, heads, levels, 1 + local_bits + b, b),
            out_shape=shape(tokens, columns),
            in_specs=[SMEM] + [VMEM] * 4,
            out_specs=VMEM,
            input_output_aliases={4: 0},
            compiler_params=params,
            cost_estimate=cost(2),
        )(me, q_all, share, states[b], acc)

    b = context_bits - 1
    span, _ = spans(heads, columns)
    return pl.pallas_call(
        functools.partial(last_kernel, heads, levels, 1 + local_bits + b, b),
        out_shape=shape(tokens, columns, dtype=BF16),
        in_specs=[SMEM] + [VMEM] * 4,
        out_specs=HBM,
        scratch_shapes=[
            pltpu.VMEM((tokens, columns), BF16),
            pltpu.SemaphoreType.DMA((heads // span,)),
        ],
        compiler_params=params,
        name="last",
    )(me, q_all, share, states[b], acc)


def solution(mesh):
    placed = (
        P(("ctx", "head"), None),
        P(("ctx", "head"), None),
        P("ctx", "head"),
        P(None, "ctx"),
        P(None, "head"),
    )
    return jax.shard_map(
        layer, mesh=mesh, in_specs=placed, out_specs=P("ctx", "head"), check_vma=False
    )
```

time: 164 us -> 54.1 us (0.33)
  local copies, waits for them, and re-layouts: 79.5 us -> 0.76 us
  matrix products: 49.9 us -> 0 us
  Pallas kernels: 0 us -> 26.3 us
  blocking collectives: 16.2 us -> 0 us
  starting transfers between devices: 5.84 us -> 12 us
  waiting for transfers between devices: 10.9 us -> 14.6 us
    another operation x9 -> x0, local copies, waits for them, and re-layouts: 72.3 us -> none  [the longest x5 46.1 us: weigh(): part.reshape(tok_rows, head_count, head_width) * share[level][:, :, None]]
    dot_general x10 -> x0, matrix products: 49.9 us -> none  [the longest x3 19.9 us: local(): jnp.dot(q_whole, cumulative_memory, preferred_element_type=jnp.float32)]
    pallas_call x0 -> x7, Pallas kernels: none -> 26.3 us  [the longest x1 9.17 us: layer(): pl.pallas_call(functools.partial(local_kernel, count, heads, levels), out...]
    all_gather x2 -> x0, blocking collectives: 16.2 us -> none  [the longest x1 9 us: local(): lax.all_gather(keys, 'head', axis=0, tiled=True)]
    convert_element_type x1 -> x0, local copies, waits for them, and re-layouts: 6.4 us -> none  [local(): return total.astype(jnp.bfloat16)]
    ppermute x3 -> x9, starting transfers between devices: 5.84 us -> 12 us  [exchanged(): return lax.ppermute(value, axis, pairs)]
    ppermute x3 -> x9, waiting for transfers between devices: 10.9 us -> 14.6 us  [exchanged(): return lax.ppermute(value, axis, pairs)]
  transfers between devices with their start and end apart: 3 -> 9, of which waited for: 1 -> 4; matrix products, arithmetic and copies ran while one was open for 63% -> 2% of each run, Pallas kernels for 0% -> 40%
where the time goes in v2:
time: 54.1 us; the launch traced here: 53.9 us
  Pallas kernels  26.3 us (49%)
  waiting for transfers between devices  14.6 us (27%)
  starting transfers between devices  12 us (22%)
  local copies, waits for them, and re-layouts  0.76 us (1%)
    ppermute x9, waiting for transfers between devices, exchanged(): return lax.ppermute(value, axis, pairs)  14.6 us
    ppermute x9, starting transfers between devices, exchanged(): return lax.ppermute(value, axis, pairs)  12 us
    pallas_call x1, Pallas kernels, layer(): pl.pallas_call(functools.partial(local_kernel, count, heads, levels), out...  9.17 us
    pallas_call x2, Pallas kernels, layer(): pl.pallas_call(functools.partial(middle_kernel, heads, levels, 1 + local_...  7.68 us
    pallas_call x1, Pallas kernels, layer(): pl.pallas_call(functools.partial(last_kernel, heads, levels, 1 + local_bi...  3.9 us
    pallas_call x1, Pallas kernels, layer(): pl.pallas_call(functools.partial(early_kernel, early, heads), out_shape=(...  3.08 us
    pallas_call x2, Pallas kernels, layer(): pl.pallas_call(functools.partial(state_kernel, which), out_shape=(shape(d...  2.45 us
  transfers between devices with their start and end apart: 9, of which 4 were waited for; matrix products, arithmetic and copies ran while one was open for 2% of the time, Pallas kernels for 40%

profile of v2, /device:TPU:0, one launch (start us, length us, event | category | flops | bytes accessed | tf_op | source)
XLA Modules:
  0.0 53.9 jit_solution(2508722857780022)
XLA Ops:
  0.0 0.0 copy-start
  0.0 3.0 %collective-permute-start.1 = (bf16[512,128]{1,0:T(8,128)(2,1)}, bf16[512,128]{1,0:T(8,128)(2,1)S(1)}, u32[]{:S(2)}, u32[]{:S(2)}) collective-permute-start(bf16[512,128]{1,0:T(8,128)(2,1)} %refs_3_.1), channel_id=1, source_target_pairs={{0,2},{1,3},{2,0},{3,1},{4,6},{5,7},{6,4},{7,5},{8,10},{9,11},{10,... | collective-permute-start | bytes 393224 | tf_op jit(solution)/shard_map/ppermute | solution.py:22
  3.0 0.0 collective-permute-start
  3.0 0.8 %copy.8.table_ref = f32[16,8]{1,0:T(8,128)S(1)} copy(f32[16,8]{0,1:T(8,128)} %param.9) | data formatting | bytes 1024 | tf_op args[4]
  3.8 2.9 %collective-permute-done.1.refs_2_.refs_0_ = bf16[512,128]{1,0:T(8,128)(2,1)S(1)} collective-permute-done((bf16[512,128]{1,0:T(8,128)(2,1)}, bf16[512,128]{1,0:T(8,128)(2,1)S(1)}, u32[]{:S(2)}, u32[]{:S(2)}) %collective-permute-start.1) | collective-permute-done | bytes 131104 | tf_op jit(solution)/shard_map/ppermute | solution.py:22
  6.7 0.0 collective-permute-start.2
  6.7 0.1 pad_add_fusion.me_ref
  6.8 0.0 collective-permute-done.refs_0_.refs_1_
  6.8 3.1 %early.1 = (bf16[512,128]{1,0:T(8,128)(2,1)S(1)}, bf16[512,128]{1,0:T(8,128)(2,1)S(1)}, bf16[2048,1024]{1,0:T(8,128)(2,1)S(1)}, f32[128,1024]{1,0:T(8,128)S(1)}, bf16[2048,128]{1,0:T(8,128)(2,1)S(1)}) custom-call(s32[2]{0:T(128)S(1)} %pad_add_fusion.me_ref, f32[16,8]{1,0:T(8,128)S(1)} %copy.8.table_ref, ...), custom_call_target="tpu_custom_call" | custom-call | flops 268435456 | bytes 4194304 | tf_op jit(solution)/shard_map/early/pallas_call | solution.py:250
  9.9 1.6 %state.2 = (f32[128,1024]{1,0:T(8,128)S(1)}, bf16[128,1024]{1,0:T(8,128)(2,1)}) custom-call(s32[2]{0:T(128)S(1)} %pad_add_fusion.me_ref, bf16[512,128]{1,0:T(8,128)(2,1)S(1)} %collective-permute-done.1.refs_2_.refs_0_, bf16[2048,1024]{1,0:T(8,128)(2,1)S(1)} %get-tuple-element.17.refs_8_.refs_1_, f32[128,1024]{1,0:T(8,128)S(1)} %get-tuple-element.20.refs_2_), custom_call_target="tpu_custom_call" | custom-call | tf_op jit(solution)/shard_map/state/pallas_call | solution.py:275
  11.5 0.0 collective-permute-done.2.refs_3_.refs_0_
  11.5 0.9 %state.3 = (f32[128,1024]{1,0:T(8,128)S(1)}, bf16[128,1024]{1,0:T(8,128)(2,1)S(1)}) custom-call(s32[2]{0:T(128)S(1)} %pad_add_fusion.me_ref, bf16[512,128]{1,0:T(8,128)(2,1)S(1)} %collective-permute-done.2.refs_3_.refs_0_, bf16[2048,1024]{1,0:T(8,128)(2,1)S(1)} %get-tuple-element.17.refs_8_.refs_1_, f32[128,1024]{1,0:T(8,128)S(1)} %get-tuple-element.21.refs_2_), custom_call_target="tpu_custom_call" | custom-call | tf_op jit(solution)/shard_map/state/pallas_call | solution.py:275
  12.3 1.8 %collective-permute-start.6 = (bf16[128,1024]{1,0:T(8,128)(2,1)S(1)}, bf16[128,1024]{1,0:T(8,128)(2,1)S(1)}, u32[]{:S(2)}, u32[]{:S(2)}) collective-permute-start(bf16[128,1024]{1,0:T(8,128)(2,1)S(1)} %get-tuple-element.23), channel_id=1, source_target_pairs={{0,4},{4,0},{8,12},{12,8},{16,20},{20,16},{24,28},{28,24},{1,5},{5... | collective-permute-start | bytes 786440 | tf_op jit(solution)/shard_map/ppermute | solution.py:22
  14.1 7.0 %collective-permute-done.6.state_ref = bf16[128,1024]{1,0:T(8,128)(2,1)S(1)} collective-permute-done((bf16[128,1024]{1,0:T(8,128)(2,1)S(1)}, bf16[128,1024]{1,0:T(8,128)(2,1)S(1)}, u32[]{:S(2)}, u32[]{:S(2)}) %collective-permute-start.6) | collective-permute-done | bytes 262176 | tf_op jit(solution)/shard_map/ppermute | solution.py:22
  21.1 0.1 fusion
  21.2 1.9 %collective-permute-start.7 = (bf16[128,1024]{1,0:T(8,128)(2,1)S(1)}, bf16[128,1024]{1,0:T(8,128)(2,1)S(1)}, u32[]{:S(2)}, u32[]{:S(2)}) collective-permute-start(bf16[128,1024]{1,0:T(8,128)(2,1)S(1)} %fusion), channel_id=1, source_target_pairs={{0,8},{4,12},{8,0},{12,4},{16,24},{20,28},{24,16},{28,20},{1,9},{5... | collective-permute-start | bytes 786440 | tf_op jit(solution)/shard_map/ppermute | solution.py:22
  23.0 0.0 copy-done
  23.0 1.5 %collective-permute-start.4 = (bf16[512,128]{1,0:T(8,128)(2,1)S(1)}, bf16[512,128]{1,0:T(8,128)(2,1)S(1)}, u32[]{:S(2)}, u32[]{:S(2)}) collective-permute-start(bf16[512,128]{1,0:T(8,128)(2,1)S(1)} %copy-done), channel_id=1, source_target_pairs={{0,2},{1,3},{2,0},{3,1},{4,6},{5,7},{6,4},{7,5},{8,10},{9,11},{10,... | collective-permute-start | bytes 393224 | tf_op jit(solution)/shard_map/ppermute | solution.py:22
  24.6 0.0 collective-permute-start.3
  24.6 3.4 %collective-permute-done.4.refs_6_ = bf16[512,128]{1,0:T(8,128)(2,1)S(1)} collective-permute-done((bf16[512,128]{1,0:T(8,128)(2,1)S(1)}, bf16[512,128]{1,0:T(8,128)(2,1)S(1)}, u32[]{:S(2)}, u32[]{:S(2)}) %collective-permute-start.4) | collective-permute-done | bytes 131104 | tf_op jit(solution)/shard_map/ppermute | solution.py:22
  28.0 0.0 collective-permute-start.5
  28.0 1.1 %collective-permute-done.7.state_ref = bf16[128,1024]{1,0:T(8,128)(2,1)S(1)} collective-permute-done((bf16[128,1024]{1,0:T(8,128)(2,1)S(1)}, bf16[128,1024]{1,0:T(8,128)(2,1)S(1)}, u32[]{:S(2)}, u32[]{:S(2)}) %collective-permute-start.7) | collective-permute-done | bytes 262176 | tf_op jit(solution)/shard_map/ppermute | solution.py:22
  29.2 0.1 add_convert_fusion
  29.3 3.8 %collective-permute-start.8 = (bf16[128,1024]{1,0:T(8,128)(2,1)S(1)}, bf16[128,1024]{1,0:T(8,128)(2,1)S(1)}, u32[]{:S(2)}, u32[]{:S(2)}) collective-permute-start(bf16[128,1024]{1,0:T(8,128)(2,1)S(1)} %add_convert_fusion), channel_id=1, source_target_pairs={{0,24},{4,28},{8,16},{12,20},{16,8},{20,12},{24,0},{28,4},{1,25},{... | collective-permute-start | bytes 786440 | tf_op jit(solution)/shard_map/ppermute | solution.py:22
  33.1 0.0 collective-permute-done.3.refs_5_
  33.1 0.0 collective-permute-done.5.refs_7_
  33.1 9.2 %near.1 = (f32[2048,1024]{1,0:T(8,128)S(1)}, bf16[2048,128]{1,0:T(8,128)(2,1)S(1)}) custom-call(s32[2]{0:T(128)S(1)} %pad_add_fusion.me_ref, bf16[512,128]{1,0:T(8,128)(2,1)S(1)} %get-tuple-element.15.refs_0_, bf16[512,128]{1,0:T(8,128)(2,1)S(1)} %collective-permute-done.refs_0_.refs_1_, bf16[512,128]{1,0:T(8,128)(2,1)S(1)} %collective-permute-done.1.refs_2_.refs_0_, ...), custom_call_target="tpu_custom_call" | custom-call | flops 1073741824 | bytes 4194304 | tf_op jit(solution)/shard_map/near/pallas_call | solution.py:293
  42.3 3.8 %shard_map.55.acc_ref = f32[2048,1024]{1,0:T(8,128)S(1)} custom-call(s32[2]{0:T(128)S(1)} %pad_add_fusion.me_ref, bf16[2048,128]{1,0:T(8,128)(2,1)S(1)} %get-tuple-element.19.q_ref, bf16[2048,128]{1,0:T(8,128)(2,1)S(1)} %get-tuple-element.18.refs_9_.share_ref, ...), custom_call_target="tpu_custom_call", output_to_operand_aliasing={{}: (4, {})} | custom-call | flops 536870912 | bytes 4194304 | tf_op jit(solution)/shard_map/pallas_call | solution.py:305
  46.1 3.8 %shard_map.56.acc_ref = f32[2048,1024]{1,0:T(8,128)S(1)} custom-call(s32[2]{0:T(128)S(1)} %pad_add_fusion.me_ref, bf16[2048,128]{1,0:T(8,128)(2,1)S(1)} %get-tuple-element.19.q_ref, bf16[2048,128]{1,0:T(8,128)(2,1)S(1)} %get-tuple-element.18.refs_9_.share_ref, ...), custom_call_target="tpu_custom_call", output_to_operand_aliasing={{}: (4, {})} | custom-call | flops 536870912 | bytes 4194304 | tf_op jit(solution)/shard_map/pallas_call | solution.py:305
  50.0 0.0 collective-permute-done.8.state_ref
  50.0 3.9 %last.1 = bf16[2048,1024]{1,0:T(8,128)(2,1)} custom-call(s32[2]{0:T(128)S(1)} %pad_add_fusion.me_ref, bf16[2048,128]{1,0:T(8,128)(2,1)S(1)} %get-tuple-element.19.q_ref, bf16[2048,128]{1,0:T(8,128)(2,1)S(1)} %get-tuple-element.18.refs_9_.share_ref, bf16[128,1024]{1,0:T(8,128)(2,1)S(1)} %collective-permute-done.8.state_ref, f32[2048,1024]{1,0:T(8,128)S(1)} %shard_map.56.acc_ref), custom_call_target="tpu_custom_call" | custom-call | tf_op jit(solution)/shard_map/last/pallas_call | solution.py:317
Async XLA Ops:
  0.0 23.0 %copy-start = (bf16[512,128]{1,0:T(8,128)(2,1)S(1)}, bf16[512,128]{1,0:T(8,128)(2,1)}, u32[]{:S(2)}) copy-start(bf16[512,128]{1,0:T(8,128)(2,1)} %refs_2_.1) | copy-start | bytes 393220
  0.0 6.7 %collective-permute-start.1 = (bf16[512,128]{1,0:T(8,128)(2,1)}, bf16[512,128]{1,0:T(8,128)(2,1)S(1)}, u32[]{:S(2)}, u32[]{:S(2)}) collective-permute-start(bf16[512,128]{1,0:T(8,128)(2,1)} %refs_3_.1), channel_id=1, source_target_pairs={{0,2},{1,3},{2,0},{3,1},{4,6},{5,7},{6,4},{7,5},{8,10},{9,11},{10,... | collective-permute-start | bytes 393224 | tf_op jit(solution)/shard_map/ppermute | solution.py:22
  3.0 3.8 %collective-permute-start = (bf16[512,128]{1,0:T(8,128)(2,1)}, bf16[512,128]{1,0:T(8,128)(2,1)S(1)}, u32[]{:S(2)}, u32[]{:S(2)}) collective-permute-start(bf16[512,128]{1,0:T(8,128)(2,1)} %refs_3_.1), channel_id=1, source_target_pairs={{0,1},{1,0},{2,3},{3,2},{4,5},{5,4},{6,7},{7,6},{8,9},{9,8},{10,11... | collective-permute-start | bytes 393224 | tf_op jit(solution)/shard_map/ppermute | solution.py:22
  6.7 4.8 %collective-permute-start.2 = (bf16[512,128]{1,0:T(8,128)(2,1)S(1)}, bf16[512,128]{1,0:T(8,128)(2,1)S(1)}, u32[]{:S(2)}, u32[]{:S(2)}) collective-permute-start(bf16[512,128]{1,0:T(8,128)(2,1)S(1)} %collective-permute-done.1.refs_2_.refs_0_), channel_id=1, source_target_pairs={{0,1},{1,0},{2,3},{3,2},{4,5},{5,4},{6,7},{7,6},{8,9},{9,8},{10,11... | collective-permute-start | bytes 393224 | tf_op jit(solution)/shard_map/ppermute | solution.py:22
  12.3 8.8 %collective-permute-start.6 = (bf16[128,1024]{1,0:T(8,128)(2,1)S(1)}, bf16[128,1024]{1,0:T(8,128)(2,1)S(1)}, u32[]{:S(2)}, u32[]{:S(2)}) collective-permute-start(bf16[128,1024]{1,0:T(8,128)(2,1)S(1)} %get-tuple-element.23), channel_id=1, source_target_pairs={{0,4},{4,0},{8,12},{12,8},{16,20},{20,16},{24,28},{28,24},{1,5},{5... | collective-permute-start | bytes 786440 | tf_op jit(solution)/shard_map/ppermute | solution.py:22
  21.2 8.0 %collective-permute-start.7 = (bf16[128,1024]{1,0:T(8,128)(2,1)S(1)}, bf16[128,1024]{1,0:T(8,128)(2,1)S(1)}, u32[]{:S(2)}, u32[]{:S(2)}) collective-permute-start(bf16[128,1024]{1,0:T(8,128)(2,1)S(1)} %fusion), channel_id=1, source_target_pairs={{0,8},{4,12},{8,0},{12,4},{16,24},{20,28},{24,16},{28,20},{1,9},{5... | collective-permute-start | bytes 786440 | tf_op jit(solution)/shard_map/ppermute | solution.py:22
  23.0 5.0 %collective-permute-start.4 = (bf16[512,128]{1,0:T(8,128)(2,1)S(1)}, bf16[512,128]{1,0:T(8,128)(2,1)S(1)}, u32[]{:S(2)}, u32[]{:S(2)}) collective-permute-start(bf16[512,128]{1,0:T(8,128)(2,1)S(1)} %copy-done), channel_id=1, source_target_pairs={{0,2},{1,3},{2,0},{3,1},{4,6},{5,7},{6,4},{7,5},{8,10},{9,11},{10,... | collective-permute-start | bytes 393224 | tf_op jit(solution)/shard_map/ppermute | solution.py:22
  24.6 8.5 %collective-permute-start.3 = (bf16[512,128]{1,0:T(8,128)(2,1)S(1)}, bf16[512,128]{1,0:T(8,128)(2,1)S(1)}, u32[]{:S(2)}, u32[]{:S(2)}) collective-permute-start(bf16[512,128]{1,0:T(8,128)(2,1)S(1)} %copy-done), channel_id=1, source_target_pairs={{0,1},{1,0},{2,3},{3,2},{4,5},{5,4},{6,7},{7,6},{8,9},{9,8},{10,11... | collective-permute-start | bytes 393224 | tf_op jit(solution)/shard_map/ppermute | solution.py:22
  28.0 5.1 %collective-permute-start.5 = (bf16[512,128]{1,0:T(8,128)(2,1)S(1)}, bf16[512,128]{1,0:T(8,128)(2,1)S(1)}, u32[]{:S(2)}, u32[]{:S(2)}) collective-permute-start(bf16[512,128]{1,0:T(8,128)(2,1)S(1)} %collective-permute-done.4.refs_6_), channel_id=1, source_target_pairs={{0,1},{1,0},{2,3},{3,2},{4,5},{5,4},{6,7},{7,6},{8,9},{9,8},{10,11... | collective-permute-start | bytes 393224 | tf_op jit(solution)/shard_map/ppermute | solution.py:22
  29.3 20.7 %collective-permute-start.8 = (bf16[128,1024]{1,0:T(8,128)(2,1)S(1)}, bf16[128,1024]{1,0:T(8,128)(2,1)S(1)}, u32[]{:S(2)}, u32[]{:S(2)}) collective-permute-start(bf16[128,1024]{1,0:T(8,128)(2,1)S(1)} %add_convert_fusion), channel_id=1, source_target_pairs={{0,24},{4,28},{8,16},{12,20},{16,8},{20,12},{24,0},{28,4},{1,25},{... | collective-permute-start | bytes 786440 | tf_op jit(solution)/shard_map/ppermute | solution.py:22

commit v3 on v0

v3 whole, which is shorter than its diff:
```python
import functools

import jax
import jax.numpy as jnp
from jax import lax
from jax.experimental import pallas as pl
from jax.experimental.pallas import tpu as pltpu
from jax.sharding import PartitionSpec as P


GROUP = 128
F32 = jnp.float32
BF16 = jnp.bfloat16
CHAIN = 2
VMEM = pl.BlockSpec(memory_space=pltpu.VMEM)
SMEM = pl.BlockSpec(memory_space=pltpu.SMEM)
HBM = pl.BlockSpec(memory_space=pltpu.HBM)


def exchanged(value, axis, mask):
    pairs = [(source, source ^ mask) for source in range(lax.axis_size(axis))]
    return lax.ppermute(value, axis, pairs)


def dot(a, b):
    return jnp.dot(a, b, preferred_element_type=F32)


def piece_rows(me, j, rows):
    return pl.ds(pl.multiple_of((me ^ j) * rows, rows), rows)


def store_shares(rows_ref, table_ref, share_ref):
    rows = rows_ref[...]
    hits = [rows == c for c in range(table_ref.shape[1])]
    for head in range(share_ref.shape[0]):
        weights = jnp.zeros(rows.shape, F32)
        for c, hit in enumerate(hits):
            weights = jnp.where(hit, table_ref[head, c], weights)
        share_ref[head] = weights / jnp.sum(weights, axis=0, keepdims=True)


def add_pairs(k_ref, v_ref, pairs_ref, j):
    rows = k_ref.shape[0]
    pair = 2 * GROUP
    me = lax.axis_index("head") ^ j
    k_t = k_ref[...].T
    total = None
    for r in range(rows // pair):
        start = pl.multiple_of(me * rows + r * pair, pair)
        part = dot(k_t[:, r * pair : (r + 1) * pair], v_ref[pl.ds(start, pair), :])
        pairs_ref[me * (rows // pair) + r] = part
        total = part if total is None else total + part
    return total


def early_kernel(table_ref, rows_hbm, q_hbm, k_hbm, v_hbm, *refs):
    q_out, k_out, v_out, s_ref, pairs_ref, share_ref, rows_ref, sems = refs
    me = lax.axis_index("head")
    rows = k_out.shape[0]
    count = v_out.shape[0] // rows
    small = [
        pltpu.make_async_copy(source, target, sems.at[count + n])
        for n, (source, target) in enumerate(
            ((rows_hbm, rows_ref), (k_hbm, k_out), (q_hbm, q_out))
        )
    ]
    copies = []
    for j in range(count):
        at = piece_rows(me, j, rows)
        copies.append(pltpu.make_async_copy(v_hbm.at[at, :], v_out.at[at, :], sems.at[j]))
    for copy in small + copies:
        copy.start()
    small[0].wait()
    store_shares(rows_ref, table_ref, share_ref)
    small[1].wait()
    small[2].wait()
    copies[0].wait()
    s_ref[...] = add_pairs(k_out, v_out, pairs_ref, 0)
    for copy in copies[1:]:
        copy.wait()


def state_kernel(which, *refs):
    ks = refs[: len(which)]
    v_ref, before_ref, _ = refs[len(which) : len(which) + 3]
    pairs_ref, *outs = refs[len(which) + 3 :]
    s = before_ref[...]
    for j, k in zip(which, ks):
        s = s + add_pairs(k, v_ref, pairs_ref, j)
    if len(outs) == 1:
        outs[0][...] = s
        return
    width = outs[0].shape[1]
    for c in range(len(outs) // 2):
        part = s[:, c * width : (c + 1) * width]
        outs[2 * c][...] = part
        outs[2 * c + 1][...] = part.astype(BF16)


def score_kernel(count, *refs):
    ks, qs = refs[:count], refs[count : 2 * count]
    q_t, q_f, scores, k_all = refs[2 * count :]
    pair = scores.shape[1]
    for j in range(count):
        at = piece_rows(lax.axis_index("head"), j, ks[0].shape[0])
        k_all[at, :] = ks[j][...]
        turned_q = qs[j][...].T
        q_t[:, at] = turned_q
        q_f[:, at] = turned_q.astype(F32)
    source = lax.broadcasted_iota(jnp.int32, (pair, pair), 0)
    token = lax.broadcasted_iota(jnp.int32, (pair, pair), 1)
    for p in range(scores.shape[0] // pair):
        at = slice(p * pair, (p + 1) * pair)
        scores[at, :] = jnp.where(source <= token, dot(k_all[at, :], q_t[:, at]), 0.0)


def loop_heads(heads, body):
    unroll = 2 if heads % 2 == 0 else 1

    @pl.loop(0, heads // unroll)
    def _(i):
        for n in range(unroll):
            body(i * unroll + n)


def near_kernel(base, width, v_ref, pairs_ref, q_ref, scores_ref, share_ref, acc_ref):
    tokens, pair = scores_ref.shape
    group = pair // 2
    pairs = tokens // pair

    def head(i):
        h = base + i
        cols = pl.ds(pl.multiple_of(h * width, width), width)
        outs = pl.ds(pl.multiple_of(i * width, width), width)
        older = lax.broadcasted_iota(jnp.int32, (1, pair), 1) < group
        uses = [[] for _ in range(pairs)]
        subtrees = [pairs_ref[p, :, cols] for p in range(pairs - 1)]
        level, size = 2, 1
        while 2 * size <= pairs:
            for b in range(0, pairs // size, 2):
                left = subtrees[b].astype(BF16).T
                for p in range((b + 1) * size, (b + 2) * size):
                    uses[p].append((level, left))
            subtrees = [x + y for x, y in zip(subtrees[0::2], subtrees[1::2])]
            level, size = level + 1, 2 * size
        for p, used in enumerate(uses):
            at = slice(p * pair, (p + 1) * pair)
            first = slice(p * pair, p * pair + group)
            second = slice(p * pair + group, (p + 1) * pair)
            own = share_ref[h, 0:1, at]
            above = jnp.where(older, own, share_ref[h, 1:2, at])
            top = (scores_ref[first, :] * above).astype(BF16)
            low = (scores_ref[second, group:] * own[:, group:]).astype(BF16)
            bottom = jnp.concatenate([jnp.zeros((group, group), BF16), low], axis=1)
            lhs, rhs = [v_ref[at, cols].T], [top, bottom]
            for l, left in used:
                lhs.append(left)
                rhs.append((q_ref[:, at] * share_ref[h, l : l + 1, at]).astype(BF16))
            acc_ref[outs, at] = dot(jnp.concatenate(lhs, axis=1), jnp.concatenate(rhs, axis=0))

    loop_heads(acc_ref.shape[0] // width, head)


def lit(share_ref, h, level, bit, at):
    share = share_ref[h, level : level + 1, at]
    return jnp.where((lax.axis_index("ctx") >> bit & 1) == 1, share, jnp.zeros_like(share))


def middle_kernel(levels, base, width, q_ref, share_ref, *refs):
    states, (acc_ref, out_ref) = refs[:-2], refs[-2:]
    rows, tokens = acc_ref.shape
    step = min(tokens, 2 * GROUP)

    def head(i):
        cols = pl.ds(pl.multiple_of(i * width, width), width)
        lhs = jnp.concatenate([state[:, cols].T for state in states], axis=1)
        for first in range(0, tokens, step):
            at = slice(first, first + step)
            rhs = [
                (q_ref[:, at] * lit(share_ref, base + i, level, bit, at)).astype(BF16)
                for level, bit in levels
            ]
            out_ref[cols, at] = acc_ref[cols, at] + dot(lhs, jnp.concatenate(rhs, axis=0))

    loop_heads(rows // width, head)


def last_kernel(level, bit, base, width, q_ref, share_ref, state_ref, acc_ref, *refs):
    out_ref, buf, sems = refs[-3:]
    rows, tokens = acc_ref.shape
    step = min(tokens, 2 * GROUP)
    lhs = state_ref[...].T
    copies = []
    for n, first in enumerate(range(0, tokens, step)):
        at = slice(first, first + step)
        found = dot(lhs, q_ref[:, at])
        for i in range(rows // width):
            cols = slice(i * width, (i + 1) * width)
            part = lit(share_ref, base + i, level, bit, at) * found[cols, :]
            buf[at, cols] = (acc_ref[cols, at] + part).astype(BF16).T
        target = out_ref.at[at, pl.ds(base * width, rows)]
        copies.append(pltpu.make_async_copy(buf.at[at, :], target, sems.at[n]))
        copies[-1].start()
    for copy in copies:
        copy.wait()


def chunks(heads):
    return CHAIN if heads % CHAIN == 0 else 1


def layer(queries, keys, values, tier_weight_rows, level_table):
    tokens, columns = values.shape
    heads = level_table.shape[1]
    levels = tier_weight_rows.shape[0]
    width = columns // heads
    rows, depth = keys.shape
    count = lax.axis_size("head")
    context_bits = lax.axis_size("ctx").bit_length() - 1
    local_bits = (tokens // GROUP).bit_length() - 1
    chain = chunks(heads)
    part = columns // chain
    ks, qs = {0: keys}, {0: queries}
    bit = count // 2
    while bit:
        for held in (ks, qs):
            for j, piece in list(held.items()):
                held[j | bit] = exchanged(piece, "head", bit)
        bit //= 2
    ks = [ks[j] for j in range(count)]
    qs = [qs[j] for j in range(count)]

    def shape(*dims, dtype=F32):
        return jax.ShapeDtypeStruct(dims, dtype)

    def call(kernel, flops, *args, **kwargs):
        cost = pl.CostEstimate(
            flops=int(flops * tokens * depth * columns), transcendentals=0, bytes_accessed=tokens * columns
        )
        return pl.pallas_call(
            kernel,
            cost_estimate=cost,
            compiler_params=pltpu.CompilerParams(vmem_limit_bytes=24 * 2**20),
            **kwargs,
        )(*args)

    fixed = [
        pltpu.with_memory_space_constraint(a, pltpu.HBM)
        for a in (tier_weight_rows, queries, keys, values)
    ]
    pair_states = shape(tokens // (2 * GROUP), depth, columns)
    qs[0], ks[0], held, total, pair_sums, share = call(
        early_kernel,
        1,
        level_table.T,
        *fixed,
        out_shape=(
            shape(rows, depth, dtype=BF16),
            shape(rows, depth, dtype=BF16),
            shape(tokens, columns, dtype=BF16),
            shape(depth, columns),
            pair_states,
            shape(heads, levels, tokens),
        ),
        in_specs=[SMEM] + [HBM] * 4,
        out_specs=(VMEM,) * 6,
        scratch_shapes=[
            pltpu.VMEM((levels, tokens), jnp.int32),
            pltpu.SemaphoreType.DMA((count + 3,)),
        ],
    )
    split = (shape(depth, part), shape(depth, part, dtype=BF16)) * chain
    half = max(1, count // 2)
    order = list(range(count))
    steps = [w for w in (order[1:half], order[half:-1], order[-1:]) if w]
    for n, which in enumerate(steps):
        outs = split if n == len(steps) - 1 else (shape(depth, columns),)
        pair_sums, *total = call(
            functools.partial(state_kernel, which),
            0.5,
            *[ks[j] for j in which],
            held,
            total,
            pair_sums,
            out_shape=(pair_states, *outs),
            in_specs=[VMEM] * (len(which) + 3),
            out_specs=(VMEM,) * (1 + len(outs)),
            input_output_aliases={len(which) + 2: 0},
        )
        total = total[0] if len(total) == 1 else total
    sums = [total[2 * c] for c in range(chain)]
    sent = [total[2 * c + 1] for c in range(chain)]

    states = [[] for _ in range(chain)]
    for b in range(context_bits):
        mask = 2 ** (b + 1) - 2 if b else 1
        for c in range(chain):
            incoming = exchanged(sent[c], "ctx", mask)
            states[c].append(incoming)
            if b + 1 < context_bits:
                sums[c] = sums[c] + incoming.astype(F32)
                sent[c] = sums[c].astype(BF16)

    q_t, q_f, scores = call(
        functools.partial(score_kernel, count),
        0.3,
        *ks,
        *qs,
        out_shape=(
            shape(depth, tokens, dtype=BF16),
            shape(depth, tokens),
            shape(tokens, 2 * GROUP),
        ),
        in_specs=[VMEM] * (2 * count),
        out_specs=(VMEM,) * 3,
        scratch_shapes=[pltpu.VMEM((tokens, depth), BF16)],
    )
    accs = [
        call(
            functools.partial(near_kernel, c * heads // chain, width),
            4 / chain,
            held,
            pair_sums,
            q_f,
            scores,
            share,
            out_shape=shape(part, tokens),
            in_specs=[VMEM] * 5,
            out_specs=VMEM,
        )
        for c in range(chain)
    ]
    places = [(1 + local_bits + b, b) for b in range(context_bits)]
    for c in range(chain):
        accs[c] = call(
            functools.partial(middle_kernel, places[:-1], c * heads // chain, width),
            2 / chain,
            q_f,
            share,
            *states[c][:-1],
            accs[c],
            out_shape=shape(part, tokens),
            in_specs=[VMEM] * (context_bits + 2),
            out_specs=VMEM,
            input_output_aliases={context_bits + 1: 0},
        )
    out = []
    for c in range(chain):
        out = [
            call(
                functools.partial(last_kernel, *places[-1], c * heads // chain, width),
                1 / chain,
                q_t,
                share,
                states[c][-1],
                accs[c],
                *out,
                out_shape=shape(tokens, columns, dtype=BF16),
                in_specs=[VMEM] * 4 + [HBM] * len(out),
                out_specs=HBM,
                input_output_aliases={4: 0} if out else {},
                scratch_shapes=[
                    pltpu.VMEM((tokens, part), BF16),
                    pltpu.SemaphoreType.DMA((tokens // (2 * GROUP),)),
                ],
            )
        ]
    return out[0]


def solution(mesh):
    placed = (
        P(("ctx", "head"), None),
        P(("ctx", "head"), None),
        P("ctx", "head"),
        P(None, "ctx"),
        P(None, "head"),
    )
    return jax.shard_map(
        layer, mesh=mesh, in_specs=placed, out_specs=P("ctx", "head"), check_vma=False
    )
```

time: 164 us -> 43.3 us (0.26)
  local copies, waits for them, and re-layouts: 79.5 us -> 0.69 us
  matrix products: 49.9 us -> 0 us
  blocking collectives: 16.2 us -> 0 us
  Pallas kernels: 0 us -> 14.8 us
  starting transfers between devices: 5.84 us -> 18 us
  waiting for transfers between devices: 10.9 us -> 9.26 us
    another operation x9 -> x0, local copies, waits for them, and re-layouts: 72.3 us -> none  [the longest x5 46.1 us: weigh(): part.reshape(tok_rows, head_count, head_width) * share[level][:, :, None]]
    dot_general x10 -> x0, matrix products: 49.9 us -> none  [the longest x3 19.9 us: local(): jnp.dot(q_whole, cumulative_memory, preferred_element_type=jnp.float32)]
    all_gather x2 -> x0, blocking collectives: 16.2 us -> none  [the longest x1 9 us: local(): lax.all_gather(keys, 'head', axis=0, tiled=True)]
    pallas_call x0 -> x11, Pallas kernels: none -> 14.8 us  [call(): pl.pallas_call(kernel, cost_estimate=cost, compiler_params=pltpu.Compiler...]
    ppermute x3 -> x12, starting transfers between devices: 5.84 us -> 18 us  [exchanged(): return lax.ppermute(value, axis, pairs)]
    convert_element_type x1 -> x0, local copies, waits for them, and re-layouts: 6.4 us -> none  [local(): return total.astype(jnp.bfloat16)]
    ppermute x3 -> x12, waiting for transfers between devices: 10.9 us -> 9.26 us  [exchanged(): return lax.ppermute(value, axis, pairs)]
  transfers between devices with their start and end apart: 3 -> 12, of which waited for: 1 -> 4; matrix products, arithmetic and copies ran while one was open for 63% -> 0% of each run, Pallas kernels for 0% -> 30%
where the time goes in v3:
time: 43.3 us; the launch traced here: 43.1 us
  starting transfers between devices  18 us (42%)
  Pallas kernels  14.8 us (34%)
  waiting for transfers between devices  9.26 us (21%)
  local copies, waits for them, and re-layouts  0.69 us (2%)
    ppermute x12, starting transfers between devices, exchanged(): return lax.ppermute(value, axis, pairs)  18 us
    pallas_call x11, Pallas kernels, call(): pl.pallas_call(kernel, cost_estimate=cost, compiler_params=pltpu.Compiler...  14.8 us
    ppermute x12, waiting for transfers between devices, exchanged(): return lax.ppermute(value, axis, pairs)  9.26 us
  transfers between devices with their start and end apart: 12, of which 4 were waited for; matrix products, arithmetic and copies ran while one was open for 0% of the time, Pallas kernels for 30%

profile of v3, /device:TPU:0, one launch (start us, length us, event | category | flops | bytes accessed | tf_op | source)
XLA Modules:
  0.0 43.1 jit_solution(13704561332822206918)
XLA Ops:
  0.0 3.0 %collective-permute-start.1 = (bf16[512,128]{1,0:T(8,128)(2,1)}, bf16[512,128]{1,0:T(8,128)(2,1)S(1)}, u32[]{:S(2)}, u32[]{:S(2)}) collective-permute-start(bf16[512,128]{1,0:T(8,128)(2,1)} %k_hbm.1), channel_id=1, source_target_pairs={{0,2},{1,3},{2,0},{3,1},{4,6},{5,7},{6,4},{7,5},{8,10},{9,11},{10,... | collective-permute-start | bytes 393224 | tf_op jit(solution)/shard_map/ppermute | solution.py:22
  3.0 0.0 collective-permute-start.4
  3.0 0.0 collective-permute-start
  3.0 4.5 %collective-permute-done.1.refs_2_.refs_0_ = bf16[512,128]{1,0:T(8,128)(2,1)S(1)} collective-permute-done((bf16[512,128]{1,0:T(8,128)(2,1)}, bf16[512,128]{1,0:T(8,128)(2,1)S(1)}, u32[]{:S(2)}, u32[]{:S(2)}) %collective-permute-start.1) | collective-permute-done | bytes 131104 | tf_op jit(solution)/shard_map/ppermute | solution.py:22
  7.6 0.0 collective-permute-start.2
  7.6 0.5 %collective-permute-start.3 = (bf16[512,128]{1,0:T(8,128)(2,1)}, bf16[512,128]{1,0:T(8,128)(2,1)S(1)}, u32[]{:S(2)}, u32[]{:S(2)}) collective-permute-start(bf16[512,128]{1,0:T(8,128)(2,1)} %q_hbm.1), channel_id=1, source_target_pairs={{0,1},{1,0},{2,3},{3,2},{4,5},{5,4},{6,7},{7,6},{8,9},{9,8},{10,11... | collective-permute-start | bytes 393224 | tf_op jit(solution)/shard_map/ppermute | solution.py:22
  8.1 0.0 copy-start
  8.1 0.7 %copy-done = f32[16,8]{0,1:T(8,128)S(1)} copy-done((f32[16,8]{0,1:T(8,128)S(1)}, f32[16,8]{0,1:T(8,128)}, u32[]{:S(2)}) %copy-start) | copy-done | bytes 536
  8.7 3.0 %shard_map.55 = (bf16[512,128]{1,0:T(8,128)(2,1)S(1)}, bf16[512,128]{1,0:T(8,128)(2,1)S(1)}, bf16[2048,1024]{1,0:T(8,128)(2,1)S(1)}, f32[128,1024]{1,0:T(8,128)S...) custom-call(f32[8,16]{1,0:T(8,128)S(1)} %bitcast.1, s32[8,2048]{1,0:T(8,128)} %rows_hbm.1, ...), custom_call_target="tpu_custom_call" | custom-call | flops 268435456 | bytes 2097152 | tf_op jit(solution)/shard_map/pallas_call | solution.py:241
  11.8 0.0 collective-permute-done.4.refs_6_
  11.8 0.1 collective-permute-start.5
  11.9 0.0 collective-permute-done.refs_1_.refs_0_
  11.9 0.3 shard_map.57
  12.2 0.3 shard_map.58
  12.6 0.0 collective-permute-done.2.refs_3_.refs_0_
  12.6 0.4 shard_map.59
  13.0 2.1 %collective-permute-start.6 = (bf16[128,512]{1,0:T(8,128)(2,1)S(1)}, bf16[128,512]{1,0:T(8,128)(2,1)S(1)}, u32[]{:S(2)}, u32[]{:S(2)}) collective-permute-start(bf16[128,512]{1,0:T(8,128)(2,1)S(1)} %get-tuple-element.35), channel_id=1, source_target_pairs={{0,4},{4,0},{8,12},{12,8},{16,20},{20,16},{24,28},{28,24},{1,5},{5... | collective-permute-start | bytes 393224 | tf_op jit(solution)/shard_map/ppermute | solution.py:22
  15.0 0.1 collective-permute-start.9
  15.1 0.0 collective-permute-done.3.refs_5_
  15.1 0.0 collective-permute-done.5.refs_7_
  15.1 0.6 %shard_map.56 = (bf16[128,2048]{1,0:T(8,128)(2,1)S(1)}, f32[128,2048]{1,0:T(8,128)S(1)}, f32[2048,256]{1,0:T(8,128)S(1)}) custom-call(bf16[512,128]{1,0:T(8,128)(2,1)S(1)} %get-tuple-element.23.refs_0_, bf16[512,128]{1,0:T(8,128)(2,1)S(1)} %collective-permute-done.refs_1_.refs_0_, bf16[512,128]{1,0:T(8,128)(2,1)S(1)} %collective-permute-done.1.refs_2_.refs_0_, ...), custom_call_target="tpu_custom_call" | custom-call | flops 80530640 | bytes 2097152 | tf_op jit(solution)/shard_map/pallas_call | solution.py:241
  15.7 3.7 %collective-permute-done.6.refs_0_ = bf16[128,512]{1,0:T(8,128)(2,1)S(1)} collective-permute-done((bf16[128,512]{1,0:T(8,128)(2,1)S(1)}, bf16[128,512]{1,0:T(8,128)(2,1)S(1)}, u32[]{:S(2)}, u32[]{:S(2)}) %collective-permute-start.6) | collective-permute-done | bytes 131104 | tf_op jit(solution)/shard_map/ppermute | solution.py:22
  19.4 2.1 %collective-permute-start.7 = (bf16[128,512]{1,0:T(8,128)(2,1)S(1)}, bf16[128,512]{1,0:T(8,128)(2,1)S(1)}, u32[]{:S(2)}, u32[]{:S(2)}) collective-permute-start(bf16[128,512]{1,0:T(8,128)(2,1)S(1)} %fusion), channel_id=1, source_target_pairs={{0,8},{4,12},{8,0},{12,4},{16,24},{20,28},{24,16},{28,20},{1,9},{5... | collective-permute-start | bytes 393224 | tf_op jit(solution)/shard_map/ppermute | solution.py:22
  21.6 0.4 collective-permute-done.9.refs_0_
  22.0 1.9 %collective-permute-start.10 = (bf16[128,512]{1,0:T(8,128)(2,1)S(1)}, bf16[128,512]{1,0:T(8,128)(2,1)S(1)}, u32[]{:S(2)}, u32[]{:S(2)}) collective-permute-start(bf16[128,512]{1,0:T(8,128)(2,1)S(1)} %fusion.1), channel_id=1, source_target_pairs={{0,8},{4,12},{8,0},{12,4},{16,24},{20,28},{24,16},{28,20},{1,9},{5... | collective-permute-start | bytes 393224 | tf_op jit(solution)/shard_map/ppermute | solution.py:22
  23.9 0.6 %collective-permute-done.7.refs_1_ = bf16[128,512]{1,0:T(8,128)(2,1)S(1)} collective-permute-done((bf16[128,512]{1,0:T(8,128)(2,1)S(1)}, bf16[128,512]{1,0:T(8,128)(2,1)S(1)}, u32[]{:S(2)}, u32[]{:S(2)}) %collective-permute-start.7) | collective-permute-done | bytes 131104 | tf_op jit(solution)/shard_map/ppermute | solution.py:22
  24.6 4.5 %collective-permute-start.8 = (bf16[128,512]{1,0:T(8,128)(2,1)S(1)}, bf16[128,512]{1,0:T(8,128)(2,1)S(1)}, u32[]{:S(2)}, u32[]{:S(2)}) collective-permute-start(bf16[128,512]{1,0:T(8,128)(2,1)S(1)} %add_convert_fusion.1), channel_id=1, source_target_pairs={{0,24},{4,28},{8,16},{12,20},{16,8},{20,12},{24,0},{28,4},{1,25},{... | collective-permute-start | bytes 393224 | tf_op jit(solution)/shard_map/ppermute | solution.py:22
  29.1 0.0 collective-permute-done.10.refs_1_
  29.1 3.8 %collective-permute-start.11 = (bf16[128,512]{1,0:T(8,128)(2,1)S(1)}, bf16[128,512]{1,0:T(8,128)(2,1)S(1)}, u32[]{:S(2)}, u32[]{:S(2)}) collective-permute-start(bf16[128,512]{1,0:T(8,128)(2,1)S(1)} %add_convert_fusion), channel_id=1, source_target_pairs={{0,24},{4,28},{8,16},{12,20},{16,8},{20,12},{24,0},{28,4},{1,25},{... | collective-permute-start | bytes 393224 | tf_op jit(solution)/shard_map/ppermute | solution.py:22
  32.9 1.8 %shard_map.62.refs_2_ = f32[512,2048]{1,0:T(8,128)S(1)} custom-call(bf16[2048,1024]{1,0:T(8,128)(2,1)S(1)} %get-tuple-element.27.refs_1_.v_ref, f32[8,128,1024]{2,1,0:T(8,128)S(1)} %get-tuple-element.37.pairs_ref, f32[128,2048]{1,0:T(8,128)S(1)} %get-tuple-element.36.q_ref, f32[2048,256]{1,0:T(8,128)S(1)} %get-tuple-element.38.scores_ref, ...), custom_call_target="tpu_custom_call" | custom-call | flops 536870912 | bytes 2097152 | tf_op jit(solution)/shard_map/pallas_call | solution.py:241
  34.7 2.0 %shard_map.60.refs_2_ = f32[512,2048]{1,0:T(8,128)S(1)} custom-call(bf16[2048,1024]{1,0:T(8,128)(2,1)S(1)} %get-tuple-element.27.refs_1_.v_ref, f32[8,128,1024]{2,1,0:T(8,128)S(1)} %get-tuple-element.37.pairs_ref, f32[128,2048]{1,0:T(8,128)S(1)} %get-tuple-element.36.q_ref, f32[2048,256]{1,0:T(8,128)S(1)} %get-tuple-element.38.scores_ref, ...), custom_call_target="tpu_custom_call" | custom-call | flops 536870912 | bytes 2097152 | tf_op jit(solution)/shard_map/pallas_call | solution.py:241
  36.7 1.4 %shard_map.61.acc_ref = f32[512,2048]{1,0:T(8,128)S(1)} custom-call(f32[128,2048]{1,0:T(8,128)S(1)} %get-tuple-element.36.q_ref, f32[8,8,2048]{2,1,0:T(8,128)S(1)} %get-tuple-element.26.share_ref, bf16[128,512]{1,0:T(8,128)(2,1)S(1)} %collective-permute-done.6.refs_0_, ...), custom_call_target="tpu_custom_call", output_to_operand_aliasing={{}: (4, {})} | custom-call | flops 268435456 | bytes 2097152 | tf_op jit(solution)/shard_map/pallas_call | solution.py:241
  38.1 1.4 %shard_map.63.acc_ref = f32[512,2048]{1,0:T(8,128)S(1)} custom-call(f32[128,2048]{1,0:T(8,128)S(1)} %get-tuple-element.36.q_ref, f32[8,8,2048]{2,1,0:T(8,128)S(1)} %get-tuple-element.26.share_ref, bf16[128,512]{1,0:T(8,128)(2,1)S(1)} %collective-permute-done.9.refs_0_, ...), custom_call_target="tpu_custom_call", output_to_operand_aliasing={{}: (4, {})} | custom-call | flops 268435456 | bytes 2097152 | tf_op jit(solution)/shard_map/pallas_call | solution.py:241
  39.5 0.0 collective-permute-done.11.state_ref
  39.5 1.8 %shard_map.64.refs_0_ = bf16[2048,1024]{1,0:T(8,128)(2,1)} custom-call(bf16[128,2048]{1,0:T(8,128)(2,1)S(1)} %get-tuple-element.25.q_ref, f32[8,8,2048]{2,1,0:T(8,128)S(1)} %get-tuple-element.26.share_ref, bf16[128,512]{1,0:T(8,128)(2,1)S(1)} %collective-permute-done.11.state_ref, f32[512,2048]{1,0:T(8,128)S(1)} %shard_map.63.acc_ref), custom_call_target="tpu_custom_call" | custom-call | flops 134217728 | bytes 2097152 | tf_op jit(solution)/shard_map/pallas_call | solution.py:241
  41.3 0.0 collective-permute-done.8.state_ref
  41.3 1.8 %shard_map.65 = bf16[2048,1024]{1,0:T(8,128)(2,1)} custom-call(bf16[128,2048]{1,0:T(8,128)(2,1)S(1)} %get-tuple-element.25.q_ref, f32[8,8,2048]{2,1,0:T(8,128)S(1)} %get-tuple-element.26.share_ref, bf16[128,512]{1,0:T(8,128)(2,1)S(1)} %collective-permute-done.8.state_ref, f32[512,2048]{1,0:T(8,128)S(1)} %shard_map.61.acc_ref, ...), custom_call_target="tpu_custom_call", output_to_operand_aliasing={{}: (4, {})} | custom-call | flops 134217728 | bytes 2097152 | tf_op jit(solution)/shard_map/pallas_call | solution.py:241
  (4 shorter events, 0.1 us)
Async XLA Ops:
  0.0 7.5 %collective-permute-start.1 = (bf16[512,128]{1,0:T(8,128)(2,1)}, bf16[512,128]{1,0:T(8,128)(2,1)S(1)}, u32[]{:S(2)}, u32[]{:S(2)}) collective-permute-start(bf16[512,128]{1,0:T(8,128)(2,1)} %k_hbm.1), channel_id=1, source_target_pairs={{0,2},{1,3},{2,0},{3,1},{4,6},{5,7},{6,4},{7,5},{8,10},{9,11},{10,... | collective-permute-start | bytes 393224 | tf_op jit(solution)/shard_map/ppermute | solution.py:22
  3.0 8.8 %collective-permute-start.4 = (bf16[512,128]{1,0:T(8,128)(2,1)}, bf16[512,128]{1,0:T(8,128)(2,1)S(1)}, u32[]{:S(2)}, u32[]{:S(2)}) collective-permute-start(bf16[512,128]{1,0:T(8,128)(2,1)} %q_hbm.1), channel_id=1, source_target_pairs={{0,2},{1,3},{2,0},{3,1},{4,6},{5,7},{6,4},{7,5},{8,10},{9,11},{10,... | collective-permute-start | bytes 393224 | tf_op jit(solution)/shard_map/ppermute | solution.py:22
  3.0 8.8 %collective-permute-start = (bf16[512,128]{1,0:T(8,128)(2,1)}, bf16[512,128]{1,0:T(8,128)(2,1)S(1)}, u32[]{:S(2)}, u32[]{:S(2)}) collective-permute-start(bf16[512,128]{1,0:T(8,128)(2,1)} %k_hbm.1), channel_id=1, source_target_pairs={{0,1},{1,0},{2,3},{3,2},{4,5},{5,4},{6,7},{7,6},{8,9},{9,8},{10,11... | collective-permute-start | bytes 393224 | tf_op jit(solution)/shard_map/ppermute | solution.py:22
  7.6 5.0 %collective-permute-start.2 = (bf16[512,128]{1,0:T(8,128)(2,1)S(1)}, bf16[512,128]{1,0:T(8,128)(2,1)S(1)}, u32[]{:S(2)}, u32[]{:S(2)}) collective-permute-start(bf16[512,128]{1,0:T(8,128)(2,1)S(1)} %collective-permute-done.1.refs_2_.refs_0_), channel_id=1, source_target_pairs={{0,1},{1,0},{2,3},{3,2},{4,5},{5,4},{6,7},{7,6},{8,9},{9,8},{10,11... | collective-permute-start | bytes 393224 | tf_op jit(solution)/shard_map/ppermute | solution.py:22
  7.6 7.5 %collective-permute-start.3 = (bf16[512,128]{1,0:T(8,128)(2,1)}, bf16[512,128]{1,0:T(8,128)(2,1)S(1)}, u32[]{:S(2)}, u32[]{:S(2)}) collective-permute-start(bf16[512,128]{1,0:T(8,128)(2,1)} %q_hbm.1), channel_id=1, source_target_pairs={{0,1},{1,0},{2,3},{3,2},{4,5},{5,4},{6,7},{7,6},{8,9},{9,8},{10,11... | collective-permute-start | bytes 393224 | tf_op jit(solution)/shard_map/ppermute | solution.py:22
  8.1 0.7 %copy-start = (f32[16,8]{0,1:T(8,128)S(1)}, f32[16,8]{0,1:T(8,128)}, u32[]{:S(2)}) copy-start(f32[16,8]{0,1:T(8,128)} %param.9) | copy-start | bytes 1540
  11.8 3.3 %collective-permute-start.5 = (bf16[512,128]{1,0:T(8,128)(2,1)S(1)}, bf16[512,128]{1,0:T(8,128)(2,1)S(1)}, u32[]{:S(2)}, u32[]{:S(2)}) collective-permute-start(bf16[512,128]{1,0:T(8,128)(2,1)S(1)} %collective-permute-done.4.refs_6_), channel_id=1, source_target_pairs={{0,1},{1,0},{2,3},{3,2},{4,5},{5,4},{6,7},{7,6},{8,9},{9,8},{10,11... | collective-permute-start | bytes 393224 | tf_op jit(solution)/shard_map/ppermute | solution.py:22
  13.0 6.4 %collective-permute-start.6 = (bf16[128,512]{1,0:T(8,128)(2,1)S(1)}, bf16[128,512]{1,0:T(8,128)(2,1)S(1)}, u32[]{:S(2)}, u32[]{:S(2)}) collective-permute-start(bf16[128,512]{1,0:T(8,128)(2,1)S(1)} %get-tuple-element.35), channel_id=1, source_target_pairs={{0,4},{4,0},{8,12},{12,8},{16,20},{20,16},{24,28},{28,24},{1,5},{5... | collective-permute-start | bytes 393224 | tf_op jit(solution)/shard_map/ppermute | solution.py:22
  15.0 7.0 %collective-permute-start.9 = (bf16[128,512]{1,0:T(8,128)(2,1)S(1)}, bf16[128,512]{1,0:T(8,128)(2,1)S(1)}, u32[]{:S(2)}, u32[]{:S(2)}) collective-permute-start(bf16[128,512]{1,0:T(8,128)(2,1)S(1)} %get-tuple-element.40), channel_id=1, source_target_pairs={{0,4},{4,0},{8,12},{12,8},{16,20},{20,16},{24,28},{28,24},{1,5},{5... | collective-permute-start | bytes 393224 | tf_op jit(solution)/shard_map/ppermute | solution.py:22
  19.4 5.1 %collective-permute-start.7 = (bf16[128,512]{1,0:T(8,128)(2,1)S(1)}, bf16[128,512]{1,0:T(8,128)(2,1)S(1)}, u32[]{:S(2)}, u32[]{:S(2)}) collective-permute-start(bf16[128,512]{1,0:T(8,128)(2,1)S(1)} %fusion), channel_id=1, source_target_pairs={{0,8},{4,12},{8,0},{12,4},{16,24},{20,28},{24,16},{28,20},{1,9},{5... | collective-permute-start | bytes 393224 | tf_op jit(solution)/shard_map/ppermute | solution.py:22
  22.0 7.1 %collective-permute-start.10 = (bf16[128,512]{1,0:T(8,128)(2,1)S(1)}, bf16[128,512]{1,0:T(8,128)(2,1)S(1)}, u32[]{:S(2)}, u32[]{:S(2)}) collective-permute-start(bf16[128,512]{1,0:T(8,128)(2,1)S(1)} %fusion.1), channel_id=1, source_target_pairs={{0,8},{4,12},{8,0},{12,4},{16,24},{20,28},{24,16},{28,20},{1,9},{5... | collective-permute-start | bytes 393224 | tf_op jit(solution)/shard_map/ppermute | solution.py:22
  24.6 16.7 %collective-permute-start.8 = (bf16[128,512]{1,0:T(8,128)(2,1)S(1)}, bf16[128,512]{1,0:T(8,128)(2,1)S(1)}, u32[]{:S(2)}, u32[]{:S(2)}) collective-permute-start(bf16[128,512]{1,0:T(8,128)(2,1)S(1)} %add_convert_fusion.1), channel_id=1, source_target_pairs={{0,24},{4,28},{8,16},{12,20},{16,8},{20,12},{24,0},{28,4},{1,25},{... | collective-permute-start | bytes 393224 | tf_op jit(solution)/shard_map/ppermute | solution.py:22
  29.1 10.3 %collective-permute-start.11 = (bf16[128,512]{1,0:T(8,128)(2,1)S(1)}, bf16[128,512]{1,0:T(8,128)(2,1)S(1)}, u32[]{:S(2)}, u32[]{:S(2)}) collective-permute-start(bf16[128,512]{1,0:T(8,128)(2,1)S(1)} %add_convert_fusion), channel_id=1, source_target_pairs={{0,24},{4,28},{8,16},{12,20},{16,8},{20,12},{24,0},{28,4},{1,25},{... | collective-permute-start | bytes 393224 | tf_op jit(solution)/shard_map/ppermute | solution.py:22

commit v4 on v3

--- a/solution.py
+++ b/solution.py
@@ -11,9 +11,7 @@
 GROUP = 128
 F32 = jnp.float32
 BF16 = jnp.bfloat16
-CHAIN = 2
 VMEM = pl.BlockSpec(memory_space=pltpu.VMEM)
-SMEM = pl.BlockSpec(memory_space=pltpu.SMEM)
 HBM = pl.BlockSpec(memory_space=pltpu.HBM)
 
 
@@ -54,15 +52,15 @@
     return total
 
 
-def early_kernel(table_ref, rows_hbm, q_hbm, k_hbm, v_hbm, *refs):
-    q_out, k_out, v_out, s_ref, pairs_ref, share_ref, rows_ref, sems = refs
+def early_kernel(table_hbm, rows_hbm, q_hbm, k_hbm, v_hbm, *refs):
+    q_out, k_out, v_out, s_ref, pairs_ref, share_ref, rows_ref, table_ref, sems = refs
     me = lax.axis_index("head")
     rows = k_out.shape[0]
     count = v_out.shape[0] // rows
     small = [
         pltpu.make_async_copy(source, target, sems.at[count + n])
         for n, (source, target) in enumerate(
-            ((rows_hbm, rows_ref), (k_hbm, k_out), (q_hbm, q_out))
+            ((rows_hbm, rows_ref), (table_hbm, table_ref), (k_hbm, k_out), (q_hbm, q_out))
         )
     ]
     copies = []
@@ -72,9 +70,10 @@
     for copy in small + copies:
         copy.start()
     small[0].wait()
+    small[1].wait()
     store_shares(rows_ref, table_ref, share_ref)
-    small[1].wait()
     small[2].wait()
+    small[3].wait()
     copies[0].wait()
     s_ref[...] = add_pairs(k_out, v_out, pairs_ref, 0)
     for copy in copies[1:]:
@@ -91,11 +90,12 @@
     if len(outs) == 1:
         outs[0][...] = s
         return
-    width = outs[0].shape[1]
-    for c in range(len(outs) // 2):
-        part = s[:, c * width : (c + 1) * width]
-        outs[2 * c][...] = part
-        outs[2 * c + 1][...] = part.astype(BF16)
+    first = 0
+    for exact, rounded in zip(outs[0::2], outs[1::2]):
+        part = s[:, first : first + exact.shape[1]]
+        exact[...] = part
+        rounded[...] = part.astype(BF16)
+        first += exact.shape[1]
 
 
 def score_kernel(count, *refs):
@@ -116,12 +116,8 @@
 
 
 def loop_heads(heads, body):
-    unroll = 2 if heads % 2 == 0 else 1
-
-    @pl.loop(0, heads // unroll)
-    def _(i):
-        for n in range(unroll):
-            body(i * unroll + n)
+    for i in range(heads):
+        body(i)
 
 
 def near_kernel(base, width, v_ref, pairs_ref, q_ref, scores_ref, share_ref, acc_ref):
@@ -131,8 +127,8 @@
 
     def head(i):
         h = base + i
-        cols = pl.ds(pl.multiple_of(h * width, width), width)
-        outs = pl.ds(pl.multiple_of(i * width, width), width)
+        cols = slice(h * width, (h + 1) * width)
+        outs = slice(i * width, (i + 1) * width)
         older = lax.broadcasted_iota(jnp.int32, (1, pair), 1) < group
         uses = [[] for _ in range(pairs)]
         subtrees = [pairs_ref[p, :, cols] for p in range(pairs - 1)]
@@ -173,7 +169,7 @@
     step = min(tokens, 2 * GROUP)
 
     def head(i):
-        cols = pl.ds(pl.multiple_of(i * width, width), width)
+        cols = slice(i * width, (i + 1) * width)
         lhs = jnp.concatenate([state[:, cols].T for state in states], axis=1)
         for first in range(0, tokens, step):
             at = slice(first, first + step)
@@ -183,31 +179,49 @@
             ]
             out_ref[cols, at] = acc_ref[cols, at] + dot(lhs, jnp.concatenate(rhs, axis=0))
 
-    loop_heads(rows // width, head)
+    @pl.when((lax.axis_index("ctx") & sum(1 << bit for _, bit in levels)) != 0)
+    def _():
+        loop_heads(rows // width, head)
 
 
 def last_kernel(level, bit, base, width, q_ref, share_ref, state_ref, acc_ref, *refs):
     out_ref, buf, sems = refs[-3:]
     rows, tokens = acc_ref.shape
     step = min(tokens, 2 * GROUP)
-    lhs = state_ref[...].T
-    copies = []
-    for n, first in enumerate(range(0, tokens, step)):
-        at = slice(first, first + step)
-        found = dot(lhs, q_ref[:, at])
-        for i in range(rows // width):
-            cols = slice(i * width, (i + 1) * width)
-            part = lit(share_ref, base + i, level, bit, at) * found[cols, :]
-            buf[at, cols] = (acc_ref[cols, at] + part).astype(BF16).T
-        target = out_ref.at[at, pl.ds(base * width, rows)]
-        copies.append(pltpu.make_async_copy(buf.at[at, :], target, sems.at[n]))
-        copies[-1].start()
+    copies = [
+        pltpu.make_async_copy(
+            buf.at[first : first + step, :],
+            out_ref.at[first : first + step, pl.ds(base * width, rows)],
+            sems.at[n],
+        )
+        for n, first in enumerate(range(0, tokens, step))
+    ]
+
+    def finish(reached):
+        if reached:
+            lhs = state_ref[...].T
+        for copy, first in zip(copies, range(0, tokens, step)):
+            at = slice(first, first + step)
+            if reached:
+                found = dot(lhs, q_ref[:, at])
+            for i in range(rows // width):
+                cols = slice(i * width, (i + 1) * width)
+                total = acc_ref[cols, at]
+                if reached:
+                    total = total + share_ref[base + i, level : level + 1, at] * found[cols, :]
+                buf[at, cols] = total.astype(BF16).T
+            copy.start()
+
+    on = (lax.axis_index("ctx") >> bit & 1) == 1
+    pl.when(on)(functools.partial(finish, True))
+    pl.when(jnp.logical_not(on))(functools.partial(finish, False))
     for copy in copies:
         copy.wait()
 
 
 def chunks(heads):
-    return CHAIN if heads % CHAIN == 0 else 1
+    small = max(1, 3 * heads // 8)
+    return ((0, small), (small, heads)) if heads > 1 else ((0, 1),)
 
 
 def layer(queries, keys, values, tier_weight_rows, level_table):
@@ -219,8 +233,9 @@
     count = lax.axis_size("head")
     context_bits = lax.axis_size("ctx").bit_length() - 1
     local_bits = (tokens // GROUP).bit_length() - 1
-    chain = chunks(heads)
-    part = columns // chain
+    spans = chunks(heads)
+    chain = len(spans)
+    parts = [(b - a) * width for a, b in spans]
     ks, qs = {0: keys}, {0: queries}
     bit = count // 2
     while bit:
@@ -247,13 +262,12 @@
 
     fixed = [
         pltpu.with_memory_space_constraint(a, pltpu.HBM)
-        for a in (tier_weight_rows, queries, keys, values)
+        for a in (level_table.T, tier_weight_rows, queries, keys, values)
     ]
     pair_states = shape(tokens // (2 * GROUP), depth, columns)
     qs[0], ks[0], held, total, pair_sums, share = call(
         early_kernel,
         1,
-        level_table.T,
         *fixed,
         out_shape=(
             shape(rows, depth, dtype=BF16),
@@ -263,14 +277,15 @@
             pair_states,
             shape(heads, levels, tokens),
         ),
-        in_specs=[SMEM] + [HBM] * 4,
+        in_specs=[HBM] * 5,
         out_specs=(VMEM,) * 6,
         scratch_shapes=[
             pltpu.VMEM((levels, tokens), jnp.int32),
-            pltpu.SemaphoreType.DMA((count + 3,)),
+            pltpu.SMEM(level_table.T.shape, F32),
+            pltpu.SemaphoreType.DMA((count + 4,)),
         ],
     )
-    split = (shape(depth, part), shape(depth, part, dtype=BF16)) * chain
+    split = tuple(shape(depth, p, dtype=d) for p in parts for d in (F32, BF16))
     half = max(1, count // 2)
     order = list(range(count))
     steps = [w for w in (order[1:half], order[half:-1], order[-1:]) if w]
@@ -318,14 +333,14 @@
     )
     accs = [
         call(
-            functools.partial(near_kernel, c * heads // chain, width),
-            4 / chain,
+            functools.partial(near_kernel, spans[c][0], width),
+            4 * parts[c] / columns,
             held,
             pair_sums,
             q_f,
             scores,
             share,
-            out_shape=shape(part, tokens),
+            out_shape=shape(parts[c], tokens),
             in_specs=[VMEM] * 5,
             out_specs=VMEM,
         )
@@ -334,13 +349,13 @@
     places = [(1 + local_bits + b, b) for b in range(context_bits)]
     for c in range(chain):
         accs[c] = call(
-            functools.partial(middle_kernel, places[:-1], c * heads // chain, width),
-            2 / chain,
+            functools.partial(middle_kernel, places[:-1], spans[c][0], width),
+            2 * parts[c] / columns,
             q_f,
             share,
             *states[c][:-1],
             accs[c],
-            out_shape=shape(part, tokens),
+            out_shape=shape(parts[c], tokens),
             in_specs=[VMEM] * (context_bits + 2),
             out_specs=VMEM,
             input_output_aliases={context_bits + 1: 0},
@@ -349,8 +364,8 @@
     for c in range(chain):
         out = [
             call(
-                functools.partial(last_kernel, *places[-1], c * heads // chain, width),
-                1 / chain,
+                functools.partial(last_kernel, *places[-1], spans[c][0], width),
+                parts[c] / columns,
                 q_t,
                 share,
                 states[c][-1],
@@ -361,7 +376,7 @@
                 out_specs=HBM,
                 input_output_aliases={4: 0} if out else {},
                 scratch_shapes=[
-                    pltpu.VMEM((tokens, part), BF16),
+                    pltpu.VMEM((tokens, parts[c]), BF16),
                     pltpu.SemaphoreType.DMA((tokens // (2 * GROUP),)),
                 ],
             )

time: 43.3 us -> 40.5 us (0.935)
  the two profiles are of different devices: /device:TPU:0 before, /device:TPU:18 now
where the time goes in v4:
time: 40.5 us; the launch traced here: 40.4 us
  waiting for transfers between devices  17.8 us (44%)
  Pallas kernels  13.9 us (34%)
  starting transfers between devices  8.46 us (21%)
    ppermute x12, waiting for transfers between devices, exchanged(): return lax.ppermute(value, axis, pairs)  17.8 us
    pallas_call x11, Pallas kernels, call(): pl.pallas_call(kernel, cost_estimate=cost, compiler_params=pltpu.Compiler...  13.9 us
    ppermute x12, starting transfers between devices, exchanged(): return lax.ppermute(value, axis, pairs)  8.46 us
  transfers between devices with their start and end apart: 12, of which 6 were waited for; matrix products, arithmetic and copies ran while one was open for 0% of the time, Pallas kernels for 29%

profile of v4, /device:TPU:18, one launch (start us, length us, event | category | flops | bytes accessed | tf_op | source)
XLA Modules:
  0.0 40.4 jit_solution(3134830589406281686)
XLA Ops:
  0.0 1.5 %collective-permute-start.1 = (bf16[512,128]{1,0:T(8,128)(2,1)}, bf16[512,128]{1,0:T(8,128)(2,1)S(1)}, u32[]{:S(2)}, u32[]{:S(2)}) collective-permute-start(bf16[512,128]{1,0:T(8,128)(2,1)} %k_hbm.1), channel_id=1, source_target_pairs={{0,2},{1,3},{2,0},{3,1},{4,6},{5,7},{6,4},{7,5},{8,10},{9,11},{10,... | collective-permute-start | bytes 393224 | tf_op jit(solution)/shard_map/ppermute | solution.py:20
  1.5 0.0 collective-permute-start
  1.5 3.9 %collective-permute-done.1.refs_2_.refs_0_ = bf16[512,128]{1,0:T(8,128)(2,1)S(1)} collective-permute-done((bf16[512,128]{1,0:T(8,128)(2,1)}, bf16[512,128]{1,0:T(8,128)(2,1)S(1)}, u32[]{:S(2)}, u32[]{:S(2)}) %collective-permute-start.1) | collective-permute-done | bytes 131104 | tf_op jit(solution)/shard_map/ppermute | solution.py:20
  5.4 0.0 collective-permute-start.2
  5.5 1.5 %collective-permute-start.4 = (bf16[512,128]{1,0:T(8,128)(2,1)}, bf16[512,128]{1,0:T(8,128)(2,1)S(1)}, u32[]{:S(2)}, u32[]{:S(2)}) collective-permute-start(bf16[512,128]{1,0:T(8,128)(2,1)} %q_hbm.1), channel_id=1, source_target_pairs={{0,2},{1,3},{2,0},{3,1},{4,6},{5,7},{6,4},{7,5},{8,10},{9,11},{10,... | collective-permute-start | bytes 393224 | tf_op jit(solution)/shard_map/ppermute | solution.py:20
  7.0 2.4 %shard_map.55 = (bf16[512,128]{1,0:T(8,128)(2,1)S(1)}, bf16[512,128]{1,0:T(8,128)(2,1)S(1)}, bf16[2048,1024]{1,0:T(8,128)(2,1)S(1)}, f32[128,1024]{1,0:T(8,128)S...) custom-call(f32[8,16]{1,0:T(8,128)} %bitcast.1, s32[8,2048]{1,0:T(8,128)} %rows_hbm.1, ...), custom_call_target="tpu_custom_call" | custom-call | flops 268435456 | bytes 2097152 | tf_op jit(solution)/shard_map/pallas_call | solution.py:256
  9.4 0.0 collective-permute-done.refs_1_.refs_0_
  9.4 0.3 shard_map.57
  9.8 0.3 shard_map.58
  10.1 0.0 collective-permute-done.2.refs_3_.refs_0_
  10.1 0.0 copy-start
  10.1 0.4 shard_map.59
  10.5 0.6 %collective-permute-start.6 = (bf16[128,640]{1,0:T(8,128)(2,1)S(1)}, bf16[128,640]{1,0:T(8,128)(2,1)S(1)}, u32[]{:S(2)}, u32[]{:S(2)}) collective-permute-start(bf16[128,640]{1,0:T(8,128)(2,1)S(1)} %get-tuple-element.35), channel_id=1, source_target_pairs={{0,4},{4,0},{8,12},{12,8},{16,20},{20,16},{24,28},{28,24},{1,5},{5... | collective-permute-start | bytes 491528 | tf_op jit(solution)/shard_map/ppermute | solution.py:20
  11.1 0.0 copy-done
  11.1 0.2 collective-permute-start.3
  11.2 0.3 collective-permute-done.4.refs_6_
  11.6 0.0 collective-permute-start.5
  11.6 1.5 %collective-permute-start.9 = (bf16[128,384]{1,0:T(8,128)(2,1)S(1)}, bf16[128,384]{1,0:T(8,128)(2,1)S(1)}, u32[]{:S(2)}, u32[]{:S(2)}) collective-permute-start(bf16[128,384]{1,0:T(8,128)(2,1)S(1)} %get-tuple-element.40), channel_id=1, source_target_pairs={{0,4},{4,0},{8,12},{12,8},{16,20},{20,16},{24,28},{28,24},{1,5},{5... | collective-permute-start | bytes 294920 | tf_op jit(solution)/shard_map/ppermute | solution.py:20
  13.1 0.0 collective-permute-done.3.refs_5_
  13.1 0.0 collective-permute-done.5.refs_7_
  13.1 0.6 %shard_map.56 = (bf16[128,2048]{1,0:T(8,128)(2,1)S(1)}, f32[128,2048]{1,0:T(8,128)S(1)}, f32[2048,256]{1,0:T(8,128)S(1)}) custom-call(bf16[512,128]{1,0:T(8,128)(2,1)S(1)} %get-tuple-element.23.refs_0_, bf16[512,128]{1,0:T(8,128)(2,1)S(1)} %collective-permute-done.refs_1_.refs_0_, bf16[512,128]{1,0:T(8,128)(2,1)S(1)} %collective-permute-done.1.refs_2_.refs_0_, ...), custom_call_target="tpu_custom_call" | custom-call | flops 80530640 | bytes 2097152 | tf_op jit(solution)/shard_map/pallas_call | solution.py:256
  13.7 3.9 %collective-permute-done.6.refs_0_ = bf16[128,640]{1,0:T(8,128)(2,1)S(1)} collective-permute-done((bf16[128,640]{1,0:T(8,128)(2,1)S(1)}, bf16[128,640]{1,0:T(8,128)(2,1)S(1)}, u32[]{:S(2)}, u32[]{:S(2)}) %collective-permute-start.6) | collective-permute-done | bytes 163872 | tf_op jit(solution)/shard_map/ppermute | solution.py:20
  17.7 1.6 %collective-permute-start.7 = (bf16[128,640]{1,0:T(8,128)(2,1)S(1)}, bf16[128,640]{1,0:T(8,128)(2,1)S(1)}, u32[]{:S(2)}, u32[]{:S(2)}) collective-permute-start(bf16[128,640]{1,0:T(8,128)(2,1)S(1)} %fusion), channel_id=1, source_target_pairs={{0,8},{4,12},{8,0},{12,4},{16,24},{20,28},{24,16},{28,20},{1,9},{5... | collective-permute-start | bytes 491528 | tf_op jit(solution)/shard_map/ppermute | solution.py:20
  19.3 0.0 collective-permute-done.9.refs_0_
  19.3 1.3 %collective-permute-start.10 = (bf16[128,384]{1,0:T(8,128)(2,1)S(1)}, bf16[128,384]{1,0:T(8,128)(2,1)S(1)}, u32[]{:S(2)}, u32[]{:S(2)}) collective-permute-start(bf16[128,384]{1,0:T(8,128)(2,1)S(1)} %fusion.1), channel_id=1, source_target_pairs={{0,8},{4,12},{8,0},{12,4},{16,24},{20,28},{24,16},{28,20},{1,9},{5... | collective-permute-start | bytes 294920 | tf_op jit(solution)/shard_map/ppermute | solution.py:20
  20.6 4.0 %collective-permute-done.7.refs_1_ = bf16[128,640]{1,0:T(8,128)(2,1)S(1)} collective-permute-done((bf16[128,640]{1,0:T(8,128)(2,1)S(1)}, bf16[128,640]{1,0:T(8,128)(2,1)S(1)}, u32[]{:S(2)}, u32[]{:S(2)}) %collective-permute-start.7) | collective-permute-done | bytes 163872 | tf_op jit(solution)/shard_map/ppermute | solution.py:20
  24.6 0.1 add_convert_fusion
  24.7 0.1 collective-permute-start.8
  24.7 2.0 %collective-permute-done.10.refs_1_ = bf16[128,384]{1,0:T(8,128)(2,1)S(1)} collective-permute-done((bf16[128,384]{1,0:T(8,128)(2,1)S(1)}, bf16[128,384]{1,0:T(8,128)(2,1)S(1)}, u32[]{:S(2)}, u32[]{:S(2)}) %collective-permute-start.10) | collective-permute-done | bytes 98336 | tf_op jit(solution)/shard_map/ppermute | solution.py:20
  26.8 0.1 collective-permute-start.11
  26.9 1.1 %shard_map.62.refs_2_ = f32[384,2048]{1,0:T(8,128)S(1)} custom-call(bf16[2048,1024]{1,0:T(8,128)(2,1)S(1)} %get-tuple-element.27.refs_1_.v_ref, f32[8,128,1024]{2,1,0:T(8,128)S(1)} %get-tuple-element.37.pairs_ref, f32[128,2048]{1,0:T(8,128)S(1)} %get-tuple-element.36.q_ref, f32[2048,256]{1,0:T(8,128)S(1)} %get-tuple-element.38.scores_ref, ...), custom_call_target="tpu_custom_call" | custom-call | flops 402653184 | bytes 2097152 | tf_op jit(solution)/shard_map/pallas_call | solution.py:256
  28.0 1.7 %shard_map.60.refs_2_ = f32[640,2048]{1,0:T(8,128)S(1)} custom-call(bf16[2048,1024]{1,0:T(8,128)(2,1)S(1)} %get-tuple-element.27.refs_1_.v_ref, f32[8,128,1024]{2,1,0:T(8,128)S(1)} %get-tuple-element.37.pairs_ref, f32[128,2048]{1,0:T(8,128)S(1)} %get-tuple-element.36.q_ref, f32[2048,256]{1,0:T(8,128)S(1)} %get-tuple-element.38.scores_ref, ...), custom_call_target="tpu_custom_call" | custom-call | flops 671088640 | bytes 2097152 | tf_op jit(solution)/shard_map/pallas_call | solution.py:256
  29.7 1.2 %shard_map.63.acc_ref = f32[384,2048]{1,0:T(8,128)S(1)} custom-call(f32[128,2048]{1,0:T(8,128)S(1)} %get-tuple-element.36.q_ref, f32[8,8,2048]{2,1,0:T(8,128)S(1)} %get-tuple-element.26.share_ref, bf16[128,384]{1,0:T(8,128)(2,1)S(1)} %collective-permute-done.9.refs_0_, ...), custom_call_target="tpu_custom_call", output_to_operand_aliasing={{}: (4, {})} | custom-call | flops 201326592 | bytes 2097152 | tf_op jit(solution)/shard_map/pallas_call | solution.py:256
  30.9 3.7 %collective-permute-done.11.state_ref = bf16[128,384]{1,0:T(8,128)(2,1)S(1)} collective-permute-done((bf16[128,384]{1,0:T(8,128)(2,1)S(1)}, bf16[128,384]{1,0:T(8,128)(2,1)S(1)}, u32[]{:S(2)}, u32[]{:S(2)}) %collective-permute-start.11) | collective-permute-done | bytes 98336 | tf_op jit(solution)/shard_map/ppermute | solution.py:20
  34.6 1.6 %shard_map.64.refs_0_ = bf16[2048,1024]{1,0:T(8,128)(2,1)} custom-call(bf16[128,2048]{1,0:T(8,128)(2,1)S(1)} %get-tuple-element.25.q_ref, f32[8,8,2048]{2,1,0:T(8,128)S(1)} %get-tuple-element.26.share_ref, bf16[128,384]{1,0:T(8,128)(2,1)S(1)} %collective-permute-done.11.state_ref, f32[384,2048]{1,0:T(8,128)S(1)} %shard_map.63.acc_ref), custom_call_target="tpu_custom_call" | custom-call | flops 100663296 | bytes 2097152 | tf_op jit(solution)/shard_map/pallas_call | solution.py:256
  36.2 2.1 %shard_map.61.acc_ref = f32[640,2048]{1,0:T(8,128)S(1)} custom-call(f32[128,2048]{1,0:T(8,128)S(1)} %get-tuple-element.36.q_ref, f32[8,8,2048]{2,1,0:T(8,128)S(1)} %get-tuple-element.26.share_ref, bf16[128,640]{1,0:T(8,128)(2,1)S(1)} %collective-permute-done.6.refs_0_, ...), custom_call_target="tpu_custom_call", output_to_operand_aliasing={{}: (4, {})} | custom-call | flops 335544320 | bytes 2097152 | tf_op jit(solution)/shard_map/pallas_call | solution.py:256
  38.4 0.0 collective-permute-done.8.state_ref
  38.4 2.0 %shard_map.65 = bf16[2048,1024]{1,0:T(8,128)(2,1)} custom-call(bf16[128,2048]{1,0:T(8,128)(2,1)S(1)} %get-tuple-element.25.q_ref, f32[8,8,2048]{2,1,0:T(8,128)S(1)} %get-tuple-element.26.share_ref, bf16[128,640]{1,0:T(8,128)(2,1)S(1)} %collective-permute-done.8.state_ref, f32[640,2048]{1,0:T(8,128)S(1)} %shard_map.61.acc_ref, ...), custom_call_target="tpu_custom_call", output_to_operand_aliasing={{}: (4, {})} | custom-call | flops 167772160 | bytes 2097152 | tf_op jit(solution)/shard_map/pallas_call | solution.py:256
  (3 shorter events, 0.1 us)
Async XLA Ops:
  0.0 5.4 %collective-permute-start.1 = (bf16[512,128]{1,0:T(8,128)(2,1)}, bf16[512,128]{1,0:T(8,128)(2,1)S(1)}, u32[]{:S(2)}, u32[]{:S(2)}) collective-permute-start(bf16[512,128]{1,0:T(8,128)(2,1)} %k_hbm.1), channel_id=1, source_target_pairs={{0,2},{1,3},{2,0},{3,1},{4,6},{5,7},{6,4},{7,5},{8,10},{9,11},{10,... | collective-permute-start | bytes 393224 | tf_op jit(solution)/shard_map/ppermute | solution.py:20
  1.5 7.9 %collective-permute-start = (bf16[512,128]{1,0:T(8,128)(2,1)}, bf16[512,128]{1,0:T(8,128)(2,1)S(1)}, u32[]{:S(2)}, u32[]{:S(2)}) collective-permute-start(bf16[512,128]{1,0:T(8,128)(2,1)} %k_hbm.1), channel_id=1, source_target_pairs={{0,1},{1,0},{2,3},{3,2},{4,5},{5,4},{6,7},{7,6},{8,9},{9,8},{10,11... | collective-permute-start | bytes 393224 | tf_op jit(solution)/shard_map/ppermute | solution.py:20
  5.4 4.7 %collective-permute-start.2 = (bf16[512,128]{1,0:T(8,128)(2,1)S(1)}, bf16[512,128]{1,0:T(8,128)(2,1)S(1)}, u32[]{:S(2)}, u32[]{:S(2)}) collective-permute-start(bf16[512,128]{1,0:T(8,128)(2,1)S(1)} %collective-permute-done.1.refs_2_.refs_0_), channel_id=1, source_target_pairs={{0,1},{1,0},{2,3},{3,2},{4,5},{5,4},{6,7},{7,6},{8,9},{9,8},{10,11... | collective-permute-start | bytes 393224 | tf_op jit(solution)/shard_map/ppermute | solution.py:20
  5.5 6.1 %collective-permute-start.4 = (bf16[512,128]{1,0:T(8,128)(2,1)}, bf16[512,128]{1,0:T(8,128)(2,1)S(1)}, u32[]{:S(2)}, u32[]{:S(2)}) collective-permute-start(bf16[512,128]{1,0:T(8,128)(2,1)} %q_hbm.1), channel_id=1, source_target_pairs={{0,2},{1,3},{2,0},{3,1},{4,6},{5,7},{6,4},{7,5},{8,10},{9,11},{10,... | collective-permute-start | bytes 393224 | tf_op jit(solution)/shard_map/ppermute | solution.py:20
  10.1 1.0 %copy-start = (bf16[512,128]{1,0:T(8,128)(2,1)S(1)}, bf16[512,128]{1,0:T(8,128)(2,1)}, u32[]{:S(2)}) copy-start(bf16[512,128]{1,0:T(8,128)(2,1)} %q_hbm.1) | copy-start | bytes 393220
  10.5 7.1 %collective-permute-start.6 = (bf16[128,640]{1,0:T(8,128)(2,1)S(1)}, bf16[128,640]{1,0:T(8,128)(2,1)S(1)}, u32[]{:S(2)}, u32[]{:S(2)}) collective-permute-start(bf16[128,640]{1,0:T(8,128)(2,1)S(1)} %get-tuple-element.35), channel_id=1, source_target_pairs={{0,4},{4,0},{8,12},{12,8},{16,20},{20,16},{24,28},{28,24},{1,5},{5... | collective-permute-start | bytes 491528 | tf_op jit(solution)/shard_map/ppermute | solution.py:20
  11.1 2.0 %collective-permute-start.3 = (bf16[512,128]{1,0:T(8,128)(2,1)S(1)}, bf16[512,128]{1,0:T(8,128)(2,1)S(1)}, u32[]{:S(2)}, u32[]{:S(2)}) collective-permute-start(bf16[512,128]{1,0:T(8,128)(2,1)S(1)} %copy-done), channel_id=1, source_target_pairs={{0,1},{1,0},{2,3},{3,2},{4,5},{5,4},{6,7},{7,6},{8,9},{9,8},{10,11... | collective-permute-start | bytes 393224 | tf_op jit(solution)/shard_map/ppermute | solution.py:20
  11.6 1.5 %collective-permute-start.5 = (bf16[512,128]{1,0:T(8,128)(2,1)S(1)}, bf16[512,128]{1,0:T(8,128)(2,1)S(1)}, u32[]{:S(2)}, u32[]{:S(2)}) collective-permute-start(bf16[512,128]{1,0:T(8,128)(2,1)S(1)} %collective-permute-done.4.refs_6_), channel_id=1, source_target_pairs={{0,1},{1,0},{2,3},{3,2},{4,5},{5,4},{6,7},{7,6},{8,9},{9,8},{10,11... | collective-permute-start | bytes 393224 | tf_op jit(solution)/shard_map/ppermute | solution.py:20
  11.6 7.7 %collective-permute-start.9 = (bf16[128,384]{1,0:T(8,128)(2,1)S(1)}, bf16[128,384]{1,0:T(8,128)(2,1)S(1)}, u32[]{:S(2)}, u32[]{:S(2)}) collective-permute-start(bf16[128,384]{1,0:T(8,128)(2,1)S(1)} %get-tuple-element.40), channel_id=1, source_target_pairs={{0,4},{4,0},{8,12},{12,8},{16,20},{20,16},{24,28},{28,24},{1,5},{5... | collective-permute-start | bytes 294920 | tf_op jit(solution)/shard_map/ppermute | solution.py:20
  17.7 6.9 %collective-permute-start.7 = (bf16[128,640]{1,0:T(8,128)(2,1)S(1)}, bf16[128,640]{1,0:T(8,128)(2,1)S(1)}, u32[]{:S(2)}, u32[]{:S(2)}) collective-permute-start(bf16[128,640]{1,0:T(8,128)(2,1)S(1)} %fusion), channel_id=1, source_target_pairs={{0,8},{4,12},{8,0},{12,4},{16,24},{20,28},{24,16},{28,20},{1,9},{5... | collective-permute-start | bytes 491528 | tf_op jit(solution)/shard_map/ppermute | solution.py:20
  19.3 7.4 %collective-permute-start.10 = (bf16[128,384]{1,0:T(8,128)(2,1)S(1)}, bf16[128,384]{1,0:T(8,128)(2,1)S(1)}, u32[]{:S(2)}, u32[]{:S(2)}) collective-permute-start(bf16[128,384]{1,0:T(8,128)(2,1)S(1)} %fusion.1), channel_id=1, source_target_pairs={{0,8},{4,12},{8,0},{12,4},{16,24},{20,28},{24,16},{28,20},{1,9},{5... | collective-permute-start | bytes 294920 | tf_op jit(solution)/shard_map/ppermute | solution.py:20
  24.7 13.7 %collective-permute-start.8 = (bf16[128,640]{1,0:T(8,128)(2,1)S(1)}, bf16[128,640]{1,0:T(8,128)(2,1)S(1)}, u32[]{:S(2)}, u32[]{:S(2)}) collective-permute-start(bf16[128,640]{1,0:T(8,128)(2,1)S(1)} %add_convert_fusion), channel_id=1, source_target_pairs={{0,24},{4,28},{8,16},{12,20},{16,8},{20,12},{24,0},{28,4},{1,25},{... | collective-permute-start | bytes 491528 | tf_op jit(solution)/shard_map/ppermute | solution.py:20
  26.8 7.9 %collective-permute-start.11 = (bf16[128,384]{1,0:T(8,128)(2,1)S(1)}, bf16[128,384]{1,0:T(8,128)(2,1)S(1)}, u32[]{:S(2)}, u32[]{:S(2)}) collective-permute-start(bf16[128,384]{1,0:T(8,128)(2,1)S(1)} %add_convert_fusion.1), channel_id=1, source_target_pairs={{0,24},{4,28},{8,16},{12,20},{16,8},{20,12},{24,0},{28,4},{1,25},{... | collective-permute-start | bytes 294920 | tf_op jit(solution)/shard_map/ppermute | solution.py:20
